TPU v7x, 32 devices: a whole 2x2x4 slice. The times are simulated.
32 devices in a mesh: dp: 4 (over x, core), fsdp: 8 (over z, y).
Axes of the slice: x: 2, y: 2, z: 4, core: 2. Of those that a mesh axis runs over, the one named last changes fastest.
Arguments:
- tokens: bfloat16 [32768, 768], P(('dp', 'fsdp')), may hold values from -6 to 6
- segment_ids: int32 [64, 512], P(('dp', 'fsdp')), may hold values from 0 to 7, never falling along the last dimension, each value on 1 to 160 neighbouring positions
- query_weight: bfloat16 [768, 768], P('fsdp'), may hold values from -0.21875 to 0.21875
- query_bias: bfloat16 [768], P('fsdp'), may hold values from -3 to 3
- key_weight: bfloat16 [768, 768], P('fsdp'), may hold values from -0.21875 to 0.21875
- value_weight: bfloat16 [768, 768], P('fsdp'), may hold values from -0.21875 to 0.21875
- value_bias: bfloat16 [768], P('fsdp'), may hold values from -3 to 3
- out_weight: bfloat16 [768, 768], P('fsdp'), may hold values from -0.625 to 0.625
- out_bias: bfloat16 [768], P('fsdp'), may hold values from -3 to 3
- first_gain: bfloat16 [768], P('fsdp'), may hold values from 0.25 to 1.75
- first_shift: bfloat16 [768], P('fsdp'), may hold values from -3 to 3
- expand_weight: bfloat16 [768, 3072], P('fsdp'), may hold values from -0.21875 to 0.21875
- expand_bias: bfloat16 [3072], P('fsdp'), may hold values from -3 to 3
- reduce_weight: bfloat16 [3072, 768], P('fsdp'), may hold values from -0.109375 to 0.109375
- reduce_bias: bfloat16 [768], P('fsdp'), may hold values from -3 to 3
- second_gain: bfloat16 [768], P('fsdp'), may hold values from 0.25 to 1.75
- second_shift: bfloat16 [768], P('fsdp'), may hold values from -3 to 3
- cotangent: bfloat16 [32768, 768], P(('dp', 'fsdp')), may hold values from -6 to 6
Outputs:
- output: bfloat16 [32768, 768], P(('dp', 'fsdp'))
- input_grad: float32 [32768, 768], P(('dp', 'fsdp'))
- grad_query_weight: float32 [768, 768], P('fsdp')
- grad_query_bias: float32 [768], P('fsdp')
- grad_key_weight: float32 [768, 768], P('fsdp')
- grad_value_weight: float32 [768, 768], P('fsdp')
- grad_value_bias: float32 [768], P('fsdp')
- grad_out_weight: float32 [768, 768], P('fsdp')
- grad_out_bias: float32 [768], P('fsdp')
- grad_first_gain: float32 [768], P('fsdp')
- grad_first_shift: float32 [768], P('fsdp')
- grad_expand_weight: float32 [768, 3072], P('fsdp')
- grad_expand_bias: float32 [3072], P('fsdp')
- grad_reduce_weight: float32 [3072, 768], P('fsdp')
- grad_reduce_bias: float32 [768], P('fsdp')
- grad_second_gain: float32 [768], P('fsdp')
- grad_second_shift: float32 [768], P('fsdp')
Inputs may be any that keep to these rules, and one draw needn't show every extreme that they name: `segment_ids`: within a sequence the fragment numbers never fall; every one of the 8 fragments is present, and the longest has exactly 160 tokens.
All inputs are finite; a program needn't handle non-finite values.
Results may differ from a plain program's by a relative error of at most 0.02.
Values may be sent and summed in bfloat16 or wider, within the bound.
A program may use at most 192 MiB of HBM per device.

v0:
```python
import jax
import jax.numpy as jnp
from jax import lax
from jax.sharding import PartitionSpec as P

HEADS = 12
HEAD = 64


def layer_norm(rows, gain, shift):
    average = jnp.mean(rows, axis=-1, keepdims=True)
    centered = rows - average
    rescale = lax.rsqrt(jnp.mean(centered * centered, axis=-1, keepdims=True) + 1e-12)
    normed = centered * rescale
    return (normed * gain.astype(jnp.float32) + shift.astype(jnp.float32), normed, rescale)


def norm_back(gradient, normed, rescale, gain):
    scaled = gradient * gain.astype(jnp.float32)
    inner_mean = jnp.mean(scaled * normed, axis=-1, keepdims=True)
    rows_grad = rescale * (scaled - jnp.mean(scaled, axis=-1, keepdims=True) - normed * inner_mean)
    return (rows_grad, jnp.sum(gradient * normed, axis=0), jnp.sum(gradient, axis=0))


def linear(rows, weight, bias):
    return jnp.dot(rows, weight, preferred_element_type=jnp.float32) + bias.astype(jnp.float32)


def weight_grad(rows, gradient):
    return jnp.einsum("ti,to->io", rows, gradient, preferred_element_type=jnp.float32)


def bias_grad(gradient):
    return jnp.sum(gradient.astype(jnp.float32), axis=0)


def back_rows(gradient, weight):
    return jnp.einsum("to,io->ti", gradient, weight, preferred_element_type=jnp.float32)


def gelu_slope(inner):
    normal_cdf = 0.5 * (1.0 + lax.erf(inner * 0.7071067811865476))
    density = jnp.exp(-0.5 * inner * inner) * 0.3989422804014327
    return normal_cdf + inner * density


def masked_scores(queries, key_rows, fragment):
    scaling = queries.shape[-1] ** (-0.5)
    scores = (
        jnp.einsum("qhd,khd->hqk", queries, key_rows, preferred_element_type=jnp.float32) * scaling
    )
    same_fragment = fragment[:, None] == fragment[None, :]
    return jnp.where(same_fragment[None, :, :], scores, -1000000000.0)


def attend_forward(bundle):
    queries, key_rows, value_rows, fragment = bundle
    scores = masked_scores(queries, key_rows, fragment)
    highest = jnp.max(scores, axis=-1, keepdims=True)
    lifted = jnp.exp(scores - highest)
    totals = jnp.sum(lifted, axis=-1, keepdims=True)
    weights = (lifted / totals).astype(jnp.bfloat16)
    mixed = jnp.einsum("hqk,khd->qhd", weights, value_rows, preferred_element_type=jnp.float32)
    return (mixed.astype(jnp.bfloat16), highest + jnp.log(totals))


def attend_backward(bundle):
    queries, key_rows, value_rows, fragment, mixed_grad, log_totals = bundle
    scaling = queries.shape[-1] ** (-0.5)
    weights = jnp.exp(masked_scores(queries, key_rows, fragment) - log_totals)
    value_grad = jnp.einsum(
        "hqk,qhd->khd", weights.astype(jnp.bfloat16), mixed_grad, preferred_element_type=jnp.float32
    )
    prob_grad = jnp.einsum(
        "qhd,khd->hqk", mixed_grad, value_rows, preferred_element_type=jnp.float32
    )
    score_grad = (
        weights * (prob_grad - jnp.sum(prob_grad * weights, axis=-1, keepdims=True))
    ).astype(jnp.bfloat16)
    query_grad = (
        jnp.einsum("hqk,khd->qhd", score_grad, key_rows, preferred_element_type=jnp.float32)
        * scaling
    )
    key_grad = (
        jnp.einsum("hqk,qhd->khd", score_grad, queries, preferred_element_type=jnp.float32)
        * scaling
    )
    return (
        query_grad.astype(jnp.bfloat16),
        key_grad.astype(jnp.bfloat16),
        value_grad.astype(jnp.bfloat16),
    )


def on_device(
    tokens,
    segment_ids,
    query_weight,
    query_bias,
    key_weight,
    value_weight,
    value_bias,
    out_weight,
    out_bias,
    first_gain,
    first_shift,
    expand_weight,
    expand_bias,
    reduce_weight,
    reduce_bias,
    second_gain,
    second_shift,
    cotangent,
):
    seq_count, seq_length = segment_ids.shape
    shaped = (seq_count, seq_length, HEADS, HEAD)
    attention_set = (
        lax.all_gather(query_weight, "fsdp", axis=0, tiled=True),
        lax.all_gather(query_bias, "fsdp", axis=0, tiled=True),
        lax.all_gather(key_weight, "fsdp", axis=0, tiled=True),
        lax.all_gather(value_weight, "fsdp", axis=0, tiled=True),
        lax.all_gather(value_bias, "fsdp", axis=0, tiled=True),
        lax.all_gather(out_weight, "fsdp", axis=0, tiled=True),
        lax.all_gather(out_bias, "fsdp", axis=0, tiled=True),
        lax.all_gather(first_gain, "fsdp", axis=0, tiled=True),
        lax.all_gather(first_shift, "fsdp", axis=0, tiled=True),
    )
    queries = (
        linear(tokens, attention_set[0], attention_set[1]).astype(jnp.bfloat16).reshape(shaped)
    )
    key_rows = (
        jnp.dot(tokens, attention_set[2], preferred_element_type=jnp.float32)
        .astype(jnp.bfloat16)
        .reshape(shaped)
    )
    value_rows = (
        linear(tokens, attention_set[3], attention_set[4]).astype(jnp.bfloat16).reshape(shaped)
    )
    mixed, log_totals = lax.map(attend_forward, (queries, key_rows, value_rows, segment_ids))
    mixed = mixed.reshape(tokens.shape)
    first_sum = tokens.astype(jnp.float32) + linear(mixed, attention_set[5], attention_set[6])
    hidden, first_normed, first_rescale = layer_norm(first_sum, attention_set[7], attention_set[8])
    hidden_low = hidden.astype(jnp.bfloat16)
    feed_set = (
        lax.all_gather(expand_weight, "fsdp", axis=0, tiled=True),
        lax.all_gather(expand_bias, "fsdp", axis=0, tiled=True),
        lax.all_gather(reduce_weight, "fsdp", axis=0, tiled=True),
        lax.all_gather(reduce_bias, "fsdp", axis=0, tiled=True),
        lax.all_gather(second_gain, "fsdp", axis=0, tiled=True),
        lax.all_gather(second_shift, "fsdp", axis=0, tiled=True),
    )
    inner = linear(hidden_low, feed_set[0], feed_set[1])
    active = jax.nn.gelu(inner, approximate=False).astype(jnp.bfloat16)
    second_sum = hidden + linear(active, feed_set[2], feed_set[3])
    output, second_normed, second_rescale = layer_norm(second_sum, feed_set[4], feed_set[5])
    feed_back = (
        lax.all_gather(expand_weight, "fsdp", axis=0, tiled=True),
        lax.all_gather(expand_bias, "fsdp", axis=0, tiled=True),
        lax.all_gather(reduce_weight, "fsdp", axis=0, tiled=True),
        lax.all_gather(reduce_bias, "fsdp", axis=0, tiled=True),
        lax.all_gather(second_gain, "fsdp", axis=0, tiled=True),
        lax.all_gather(second_shift, "fsdp", axis=0, tiled=True),
    )
    second_grad, grad_second_gain, grad_second_shift = norm_back(
        cotangent.astype(jnp.float32), second_normed, second_rescale, feed_back[4]
    )
    branch_grad = second_grad.astype(jnp.bfloat16)
    grad_reduce = weight_grad(active, branch_grad)
    grad_reduce_bias = bias_grad(branch_grad)
    inner_grad = (back_rows(branch_grad, feed_back[2]) * gelu_slope(inner)).astype(jnp.bfloat16)
    grad_expand = weight_grad(hidden_low, inner_grad)
    grad_expand_bias = bias_grad(inner_grad)
    hidden_grad = second_grad + back_rows(inner_grad, feed_back[0])
    feed_grads = (
        lax.psum_scatter(
            grad_expand.astype(jnp.bfloat16), "fsdp", scatter_dimension=0, tiled=True
        ).astype(jnp.float32),
        lax.psum_scatter(
            grad_expand_bias.astype(jnp.bfloat16), "fsdp", scatter_dimension=0, tiled=True
        ).astype(jnp.float32),
        lax.psum_scatter(
            grad_reduce.astype(jnp.bfloat16), "fsdp", scatter_dimension=0, tiled=True
        ).astype(jnp.float32),
        lax.psum_scatter(
            grad_reduce_bias.astype(jnp.bfloat16), "fsdp", scatter_dimension=0, tiled=True
        ).astype(jnp.float32),
        lax.psum_scatter(
            grad_second_gain.astype(jnp.bfloat16), "fsdp", scatter_dimension=0, tiled=True
        ).astype(jnp.float32),
        lax.psum_scatter(
            grad_second_shift.astype(jnp.bfloat16), "fsdp", scatter_dimension=0, tiled=True
        ).astype(jnp.float32),
    )
    attention_back = (
        lax.all_gather(query_weight, "fsdp", axis=0, tiled=True),
        lax.all_gather(query_bias, "fsdp", axis=0, tiled=True),
        lax.all_gather(key_weight, "fsdp", axis=0, tiled=True),
        lax.all_gather(value_weight, "fsdp", axis=0, tiled=True),
        lax.all_gather(value_bias, "fsdp", axis=0, tiled=True),
        lax.all_gather(out_weight, "fsdp", axis=0, tiled=True),
        lax.all_gather(out_bias, "fsdp", axis=0, tiled=True),
        lax.all_gather(first_gain, "fsdp", axis=0, tiled=True),
        lax.all_gather(first_shift, "fsdp", axis=0, tiled=True),
    )
    first_grad, grad_first_gain, grad_first_shift = norm_back(
        hidden_grad, first_normed, first_rescale, attention_back[7]
    )
    out_grad = first_grad.astype(jnp.bfloat16)
    grad_out = weight_grad(mixed, out_grad)
    grad_out_bias = bias_grad(out_grad)
    mixed_grad = back_rows(out_grad, attention_back[5]).astype(jnp.bfloat16).reshape(shaped)
    query_grad, key_grad, value_grad = lax.map(
        attend_backward, (queries, key_rows, value_rows, segment_ids, mixed_grad, log_totals)
    )
    query_grad = query_grad.reshape(tokens.shape)
    key_grad = key_grad.reshape(tokens.shape)
    value_grad = value_grad.reshape(tokens.shape)
    grad_query = weight_grad(tokens, query_grad)
    grad_query_bias = bias_grad(query_grad)
    grad_key = weight_grad(tokens, key_grad)
    grad_value = weight_grad(tokens, value_grad)
    grad_value_bias = bias_grad(value_grad)
    input_grad = (
        first_grad
        + back_rows(query_grad, attention_back[0])
        + back_rows(key_grad, attention_back[2])
        + back_rows(value_grad, attention_back[3])
    )
    attention_grads = (
        lax.psum_scatter(
            grad_query.astype(jnp.bfloat16), "fsdp", scatter_dimension=0, tiled=True
        ).astype(jnp.float32),
        lax.psum_scatter(
            grad_query_bias.astype(jnp.bfloat16), "fsdp", scatter_dimension=0, tiled=True
        ).astype(jnp.float32),
        lax.psum_scatter(
            grad_key.astype(jnp.bfloat16), "fsdp", scatter_dimension=0, tiled=True
        ).astype(jnp.float32),
        lax.psum_scatter(
            grad_value.astype(jnp.bfloat16), "fsdp", scatter_dimension=0, tiled=True
        ).astype(jnp.float32),
        lax.psum_scatter(
            grad_value_bias.astype(jnp.bfloat16), "fsdp", scatter_dimension=0, tiled=True
        ).astype(jnp.float32),
        lax.psum_scatter(
            grad_out.astype(jnp.bfloat16), "fsdp", scatter_dimension=0, tiled=True
        ).astype(jnp.float32),
        lax.psum_scatter(
            grad_out_bias.astype(jnp.bfloat16), "fsdp", scatter_dimension=0, tiled=True
        ).astype(jnp.float32),
        lax.psum_scatter(
            grad_first_gain.astype(jnp.bfloat16), "fsdp", scatter_dimension=0, tiled=True
        ).astype(jnp.float32),
        lax.psum_scatter(
            grad_first_shift.astype(jnp.bfloat16), "fsdp", scatter_dimension=0, tiled=True
        ).astype(jnp.float32),
    )
    summed = (
        lax.psum(attention_grads[0].astype(jnp.bfloat16), "dp").astype(jnp.float32),
        lax.psum(attention_grads[1].astype(jnp.bfloat16), "dp").astype(jnp.float32),
        lax.psum(attention_grads[2].astype(jnp.bfloat16), "dp").astype(jnp.float32),
        lax.psum(attention_grads[3].astype(jnp.bfloat16), "dp").astype(jnp.float32),
        lax.psum(attention_grads[4].astype(jnp.bfloat16), "dp").astype(jnp.float32),
        lax.psum(attention_grads[5].astype(jnp.bfloat16), "dp").astype(jnp.float32),
        lax.psum(attention_grads[6].astype(jnp.bfloat16), "dp").astype(jnp.float32),
        lax.psum(attention_grads[7].astype(jnp.bfloat16), "dp").astype(jnp.float32),
        lax.psum(attention_grads[8].astype(jnp.bfloat16), "dp").astype(jnp.float32),
        lax.psum(feed_grads[0].astype(jnp.bfloat16), "dp").astype(jnp.float32),
        lax.psum(feed_grads[1].astype(jnp.bfloat16), "dp").astype(jnp.float32),
        lax.psum(feed_grads[2].astype(jnp.bfloat16), "dp").astype(jnp.float32),
        lax.psum(feed_grads[3].astype(jnp.bfloat16), "dp").astype(jnp.float32),
        lax.psum(feed_grads[4].astype(jnp.bfloat16), "dp").astype(jnp.float32),
        lax.psum(feed_grads[5].astype(jnp.bfloat16), "dp").astype(jnp.float32),
    )
    return (
        output.astype(jnp.bfloat16),
        input_grad,
        summed[0],
        summed[1],
        summed[2],
        summed[3],
        summed[4],
        summed[5],
        summed[6],
        summed[7],
        summed[8],
        summed[9],
        summed[10],
        summed[11],
        summed[12],
        summed[13],
        summed[14],
    )


def solution(mesh):
    in_specs = (
        P(("dp", "fsdp"), None),
        P(("dp", "fsdp"), None),
        P("fsdp", None),
        P("fsdp"),
        P("fsdp", None),
        P("fsdp", None),
        P("fsdp"),
        P("fsdp", None),
        P("fsdp"),
        P("fsdp"),
        P("fsdp"),
        P("fsdp", None),
        P("fsdp"),
        P("fsdp", None),
        P("fsdp"),
        P("fsdp"),
        P("fsdp"),
        P(("dp", "fsdp"), None),
    )
    out_specs = (
        P(("dp", "fsdp"), None),
        P(("dp", "fsdp"), None),
        P("fsdp", None),
        P("fsdp"),
        P("fsdp", None),
        P("fsdp", None),
        P("fsdp"),
        P("fsdp", None),
        P("fsdp"),
        P("fsdp"),
        P("fsdp"),
        P("fsdp", None),
        P("fsdp"),
        P("fsdp", None),
        P("fsdp"),
        P("fsdp"),
        P("fsdp"),
    )
    return jax.shard_map(
        on_device, mesh=mesh, in_specs=in_specs, out_specs=out_specs, check_vma=False
    )
```

profile of v0, /device:TPU:11, one launch (start us, length us, event | category | flops | bytes accessed | tf_op | source)
XLA Modules:
  0.0 984.7 jit_solution(2345672940246471056)
XLA Ops:
  19.1 28.2 %all-reduce.18 = (bf16[768]{0:T(1024)(128)(2,1)S(1)}, bf16[768]{0:T(1024)(128)(2,1)S(1)}, bf16[768]{0:T(1024)(128)(2,1)S(1)}, bf16[768]{0:T(1024)(128)(2,1)S(1)}...) all-reduce(bf16[768]{0:T(1024)(128)(2,1)S(1)} %dynamic-update-slice, ...), channel_id=1, replica_groups=mesh['dp'=4,'fsdp'=8] {'fsdp'}, use_global_device_ids=true, to_apply=%add.1 | all-reduce | flops 5376 | bytes 21504
  50.0 22.4 %all-gather = bf16[8,1,384]{2,1,0:T(2,128)(2,1)S(1)} all-gather(bf16[1,1,384]{2,1,0:T(2,128)(2,1)S(1)} %reshape.227), channel_id=1, replica_groups=mesh['dp'=4,'fsdp'=8] {'fsdp'}, dimensions={0}, use_global_device_ids=true | all-gather | bytes 6912 | tf_op jit(solution)/shard_map/all_gather | solution.py:146
  83.6 9.6 all-gather.10.cloned.1.call-done
  98.2 37.1 %all-gather.12.cloned.1.call-done = bf16[768,768]{1,0:T(8,128)(2,1)} async-done(((bf16[96,768]{1,0:T(8,128)(2,1)}), bf16[768,768]{1,0:T(8,128)(2,1)}) %all-gather.12.cloned.1.call-update) | async-done | bytes 1179664 | tf_op jit(solution)/shard_map/all_gather | solution.py:120
  146.7 21.0 %while.26 = (s32[]{:T(128)}, bf16[2,512,12,64]{1,3,2,0:T(8,128)(2,1)}, f32[2,12,512,1]{2,1,3,0:T(8,128)S(1)}, bf16[2,512,12,64]{1,3,2,0:T(8,128)(2,1)}, s32[2,51...) while((s32[]{:T(128)}, ...), condition=%wide.region_3.4_spmd, body=%wide.region_0.3_spmd.sunk | while | flops 843704320 | bytes 42172508 | solution.py:139
  183.1 73.3 %all-gather.16.cloned.1.call-done = bf16[768,3072]{1,0:T(8,128)(2,1)} async-done(((bf16[96,3072]{1,0:T(8,128)(2,1)}), bf16[768,3072]{1,0:T(8,128)(2,1)}) %all-gather.16.cloned.1.call-update) | async-done | bytes 4718608 | tf_op jit(solution)/shard_map/all_gather | solution.py:145
  256.4 50.4 %fusion.59 = (bf16[1024,3072]{1,0:T(8,128)(2,1)}, f32[1024,3072]{1,0:T(8,128)}) fusion(f32[3072]{0:T(1024)S(1)} %bitcast.193, bf16[768,3072]{1,0:T(8,128)(2,1)} %all-gather.16.cloned.1.call-done, f32[1024,768]{0,1:T(8,128)} %copy-done.7, f32[768]{0:T(1024)S(1)} %convert_element_type.228, f32[768]{0:T(1024)S(1)} %convert_element_type.227, ...), kind=kOutput, calls=%fused_computation.68 | convolution fusion | flops 5043388416 | bytes 26765312 | tf_op jit(solution)/shard_map/dot_general | solution.py:26
  306.8 29.4 %all-gather.18.cloned.1.call-done = bf16[3072,768]{1,0:T(8,128)(2,1)} async-done(((bf16[384,768]{1,0:T(8,128)(2,1)}), bf16[3072,768]{1,0:T(8,128)(2,1)}) %all-gather.18.cloned.1.call-update) | async-done | bytes 4718608 | tf_op jit(solution)/shard_map/all_gather | solution.py:147
  336.2 9.4 fusion.94
  352.0 14.7 %fusion.95 = (bf16[3072]{0:T(1024)(128)(2,1)}, bf16[1024,3072]{1,0:T(8,128)(2,1)}) fusion(f32[1024,3072]{1,0:T(8,128)} %get-tuple-element.302, f32[3072]{0:T(1024)S(1)} %bitcast.194, bf16[1024,768]{0,1:T(8,128)(2,1)S(1)} %get-tuple-element.290, bf16[3072,768]{1,0:T(8,128)(2,1)S(1)} %bitcast.198), kind=kOutput, calls=%fused_computation.144 | convolution fusion | flops 4869583872 | bytes 25184256 | tf_op jit(solution)/shard_map/to,io->ti/dot_general | solution.py:38
  366.7 9.7 multiply_reduce_fusion.1
  395.9 48.5 %while.27 = (s32[]{:T(128)}, bf16[2,512,12,64]{1,3,2,0:T(8,128)(2,1)}, bf16[2,512,12,64]{1,3,2,0:T(8,128)(2,1)}, bf16[2,512,12,64]{1,3,2,0:T(8,128)(2,1)}, bf16[...) while((s32[]{:T(128)}, ...), condition=%wide.region_14.15_spmd, body=%wide.region_12.14_spmd.sunk | while | flops 2062673920 | bytes 134941968 | solution.py:212
  405.1 7.1 multiply_convert_fusion.4
  429.2 7.1 multiply_convert_fusion.4
  475.2 9.8 convolution_convert_fusion.1
  486.4 9.8 convolution_convert_fusion
  501.7 27.1 %all-reduce.17 = (bf16[768]{0:T(1024)(128)(2,1)S(1)}, bf16[768]{0:T(1024)(128)(2,1)S(1)}, bf16[768]{0:T(1024)(128)(2,1)S(1)}, bf16[768]{0:T(1024)(128)(2,1)S(1)}...) all-reduce(bf16[768]{0:T(1024)(128)(2,1)S(1)} %dynamic-update-slice, ...), channel_id=1, replica_groups=mesh['dp'=4,'fsdp'=8] {'fsdp'}, use_global_device_ids=true, to_apply=%add.7 | all-reduce | flops 9984 | bytes 39936
  529.5 13.0 %all-reduce.19 = (bf16[96]{0:T(256)(128)(2,1)S(1)}, bf16[96]{0:T(256)(128)(2,1)S(1)}, bf16[96]{0:T(256)(128)(2,1)S(1)}, bf16[96]{0:T(256)(128)(2,1)S(1)}, bf16[9...) all-reduce(bf16[96]{0:T(256)(128)(2,1)S(1)} %dynamic-slice.9, ...), channel_id=1, replica_groups=mesh['dp'=4,'fsdp'=8] {'dp'}, use_global_device_ids=true, to_apply=%region_19.20 | all-reduce | flops 1152 | bytes 4608 | tf_op jit(solution)/shard_map/psum | solution.py:260
  556.5 28.1 %reduce-scatter.21.cloned.1.call-done = bf16[96,768]{1,0:T(8,128)(2,1)} async-done(((bf16[768,768]{1,0:T(8,128)(2,1)}), bf16[96,768]{1,0:T(8,128)(2,1)}) %reduce-scatter.21.cloned.1.call-update) | async-done | bytes 147472
  586.4 65.5 %reduce-scatter.23.cloned.1.call-done = bf16[96,768]{1,0:T(8,128)(2,1)} async-done(((bf16[768,768]{1,0:T(8,128)(2,1)}), bf16[96,768]{1,0:T(8,128)(2,1)}) %reduce-scatter.23.cloned.1.call-update) | async-done | bytes 147472
  653.6 65.9 %reduce-scatter.13.cloned.1.call-done = bf16[96,768]{1,0:T(8,128)(2,1)} async-done(((bf16[768,768]{1,0:T(8,128)(2,1)}), bf16[96,768]{1,0:T(8,128)(2,1)}) %reduce-scatter.13.cloned.1.call-update) | async-done | bytes 147472 | tf_op jit(solution)/shard_map/reduce_scatter | solution.py:245
  719.6 100.4 %reduce-scatter.15.cloned.1.call-done = bf16[96,3072]{1,0:T(8,128)(2,1)} async-done(((bf16[768,3072]{1,0:T(8,128)(2,1)}), bf16[96,3072]{1,0:T(8,128)(2,1)}) %reduce-scatter.15.cloned.1.call-update) | async-done | bytes 589840 | tf_op jit(solution)/shard_map/reduce_scatter | solution.py:175
  820.0 98.9 %reduce-scatter.17.cloned.1.call-done = bf16[384,768]{1,0:T(8,128)(2,1)} async-done(((bf16[3072,768]{1,0:T(8,128)(2,1)}), bf16[384,768]{1,0:T(8,128)(2,1)}) %reduce-scatter.17.cloned.1.call-update) | async-done | bytes 589840 | tf_op jit(solution)/shard_map/reduce_scatter | solution.py:181
  933.7 36.3 %all-reduce.23.cloned.1.call-done = (bf16[96,768]{0,1:T(8,128)(2,1)}, bf16[96,768]{0,1:T(8,128)(2,1)}, bf16[96,768]{0,1:T(8,128)(2,1)}, bf16[96,768]{1,0:T(8,128...) async-done(((bf16[96,768]{0,1:T(8,128)(2,1)}, bf16[96,768]{0,1:T(8,128)(2,1)}, bf16[96,768]{0,1:T(8,128)(2,1)}, bf16[96,768]{1,0:T(8,128)(2,1)}, ...) | async-done | bytes 1769488 | tf_op jit(solution)/shard_map/psum | solution.py:259
  (307 shorter events, 213.8 us)
Async XLA Ops:
  7.2 42.8 %copy-start.53 = (bf16[384]{0:T(512)(128)(2,1)S(1)}, bf16[384]{0:T(512)(128)(2,1)}, u32[]{:S(2)}) copy-start(bf16[384]{0:T(512)(128)(2,1)} %param.34) | copy-start | bytes 2308
  7.2 66.5 %copy-start.11 = (bf16[1024,768]{1,0:T(8,128)(2,1)S(1)}, bf16[1024,768]{1,0:T(8,128)(2,1)}, u32[]{:S(2)}) copy-start(bf16[1024,768]{1,0:T(8,128)(2,1)} %param.39) | copy-start | bytes 4718596
  7.2 68.1 %all-gather.8.cloned.1.call-start = ((), (), s32[]{:S(2)}) async-start(), calls=%async_computation.6 | async-start | bytes 1327104 | tf_op jit(solution)/shard_map/all_gather | solution.py:121
  7.9 85.3 %all-gather.10.cloned.1.call-start = ((), (), s32[]{:S(2)}) async-start(), calls=%async_computation.7 | async-start | bytes 1327104 | tf_op jit(solution)/shard_map/all_gather | solution.py:118
  8.7 126.6 %all-gather.12.cloned.1.call-start = ((), (), s32[]{:S(2)}) async-start(), calls=%async_computation.8 | async-start | bytes 1327104 | tf_op jit(solution)/shard_map/all_gather | solution.py:120
  9.4 167.7 %all-gather.14.cloned.1.call-start = ((), (), s32[]{:S(2)}) async-start(), calls=%async_computation.9 | async-start | bytes 1327104 | tf_op jit(solution)/shard_map/all_gather | solution.py:123
  10.0 246.4 %all-gather.16.cloned.1.call-start = ((), (), s32[]{:S(2)}) async-start(), calls=%async_computation.10 | async-start | bytes 5308416 | tf_op jit(solution)/shard_map/all_gather | solution.py:145
  10.6 325.6 %all-gather.18.cloned.1.call-start = ((), (), s32[]{:S(2)}) async-start(), calls=%async_computation.11 | async-start | bytes 5308416 | tf_op jit(solution)/shard_map/all_gather | solution.py:147
  11.2 543.7 %reduce-scatter.19.cloned.1.call-start = ((), (), s32[]{:S(2)}) async-start(), calls=%async_computation.15 | async-start | bytes 1327104
  47.3 28.0 %copy-start.17 = (bf16[1024,768]{1,0:T(8,128)(2,1)S(1)}, bf16[1024,768]{1,0:T(8,128)(2,1)}, u32[]{:S(2)}) copy-start(bf16[1024,768]{1,0:T(8,128)(2,1)} %param.22) | copy-start | bytes 4718596
  50.0 326.4 %copy-start.40 = (f32[768]{0:T(1024)}, f32[768]{0:T(1024)S(1)}, u32[]{:S(2)}) copy-start(f32[768]{0:T(1024)S(1)} %convert_element_type.227) | copy-start | bytes 9220
  50.0 286.1 %copy-start.48 = (f32[768]{0:T(1024)}, f32[768]{0:T(1024)S(1)}, u32[]{:S(2)}) copy-start(f32[768]{0:T(1024)S(1)} %convert_element_type.228) | copy-start | bytes 9220
  181.0 195.4 %copy-start.38 = (f32[1024]{0:T(1024)}, f32[1024]{0:T(1024)S(1)}, u32[]{:S(2)}) copy-start(f32[1024]{0:T(1024)S(1)} %broadcast_multiply_fusion.5) | copy-start | bytes 12292
  183.1 193.4 %copy-start.42 = (f32[1024]{0:T(1024)}, f32[1024]{0:T(1024)S(1)}, u32[]{:S(2)}) copy-start(f32[1024]{0:T(1024)S(1)} %add_rsqrt_fusion.1) | copy-start | bytes 12292
  256.4 79.8 %copy-start.50 = (f32[768]{0:T(1024)S(1)}, f32[768]{0:T(1024)}, u32[]{:S(2)}) copy-start(f32[768]{0:T(1024)} %convert_element_type.232) | copy-start | bytes 9220
  345.6 21.1 %copy-start = (f32[1024,768]{0,1:T(8,128)}, f32[1024,768]{0,1:T(8,128)S(1)}, u32[]{:S(2)}) copy-start(f32[1024,768]{0,1:T(8,128)S(1)} %get-tuple-element.304) | copy-start | bytes 9437188
  454.0 130.7 %reduce-scatter.21.cloned.1.call-start = ((), (), s32[]{:S(2)}) async-start(), calls=%async_computation.16 | async-start | bytes 1327104
  462.4 189.5 %reduce-scatter.23.cloned.1.call-start = ((), (), s32[]{:S(2)}) async-start(), calls=%async_computation.17 | async-start | bytes 1327104
  470.7 248.9 %reduce-scatter.13.cloned.1.call-start = ((), (), s32[]{:S(2)}) async-start(), calls=%async_computation.12 | async-start | bytes 1327104 | tf_op jit(solution)/shard_map/reduce_scatter | solution.py:245
  475.1 344.9 %reduce-scatter.15.cloned.1.call-start = ((), (), s32[]{:S(2)}) async-start(), calls=%async_computation.13 | async-start | bytes 5308416 | tf_op jit(solution)/shard_map/reduce_scatter | solution.py:175
  485.0 433.8 %reduce-scatter.17.cloned.1.call-start = ((), (), s32[]{:S(2)}) async-start(), calls=%async_computation.14 | async-start | bytes 5308416 | tf_op jit(solution)/shard_map/reduce_scatter | solution.py:181
  496.3 473.8 %all-reduce.23.cloned.1.call-start = ((), (), s32[]{:S(2)}) async-start(), calls=%async_computation.18 | async-start | bytes 3833856 | tf_op jit(solution)/shard_map/psum | solution.py:259
  497.9 49.3 %copy-start.22 = (bf16[96,8,2,512]{3,1,2,0:T(8,128)(2,1)S(1)}, bf16[96,8,2,512]{3,1,2,0:T(8,128)(2,1)}, u32[]{:S(2)}) copy-start(bf16[96,8,2,512]{3,1,2,0:T(8,128)(2,1)} %copy-done.21) | copy-start | bytes 4718596
  551.8 367.1 %copy-start.10 = (f32[1024,768]{0,1:T(8,128)S(1)}, f32[1024,768]{0,1:T(8,128)}, u32[]{:S(2)}) copy-start(f32[1024,768]{0,1:T(8,128)} %copy-done.9) | copy-start | bytes 9437188
  (55 other events, 287.2 us)
Sparse Core Ops, SparseCore 0:
  10.2 40.9 all-gather.7
  53.4 39.7 all-gather.9
  95.4 39.7 all-gather.11
  137.3 39.7 all-gather.13
  179.1 77.2 all-gather.15
  258.4 77.6 all-gather.17
  454.1 63.2 reduce-scatter.18
  520.8 63.8 reduce-scatter.20
  588.1 63.7 reduce-scatter.22
  655.7 63.8 reduce-scatter.12
  723.2 96.6 reduce-scatter.14
  823.5 95.3 reduce-scatter.16
  922.2 47.7 all-reduce.22
where the time goes:
time: 995 us; the launch traced here: 985 us
  waiting for transfers between devices  553 us (56%)
  matrix products  195 us (20%)
  blocking collectives  90.7 us (9%)
  local copies, waits for them, and re-layouts  85.1 us (9%)
  other arithmetic  41.6 us (4%)
  between operations  17.1 us (2%)
    reduce_scatter x1, waiting for transfers between devices, on_device(): lax.psum_scatter(grad_expand.astype(jnp.bfloat16), 'fsdp', scatter_dimens...  100 us
    reduce_scatter x1, waiting for transfers between devices, on_device(): lax.psum_scatter(grad_reduce.astype(jnp.bfloat16), 'fsdp', scatter_dimens...  98.9 us
    unnamed x16, waiting for transfers between devices  97.4 us
    all_gather x1, waiting for transfers between devices, on_device(): lax.all_gather(expand_weight, 'fsdp', axis=0, tiled=True)  73.3 us
    dot_general x5, matrix products, linear(): jnp.dot(rows, weight, preferred_element_type=jnp.float32)  70.2 us
    reduce_scatter x1, waiting for transfers between devices, on_device(): lax.psum_scatter(grad_out.astype(jnp.bfloat16), 'fsdp', scatter_dimension...  65.9 us
    unnamed x2, blocking collectives  55.3 us
    unnamed x156, local copies, waits for them, and re-layouts  48.2 us
  transfers between devices with their start and end apart: 13, of which 11 were waited for; matrix products, arithmetic and copies ran while one was open for 19% of the time, Pallas kernels for 0%

commit v1 on v0

v1 whole, which is shorter than its diff:
```python
import jax
import jax.numpy as jnp
from jax import lax
from jax.sharding import PartitionSpec as P

HEADS = 12
HEAD = 64


def layer_norm(rows, gain, shift):
    average = jnp.mean(rows, axis=-1, keepdims=True)
    centered = rows - average
    rescale = lax.rsqrt(jnp.mean(centered * centered, axis=-1, keepdims=True) + 1e-12)
    normed = centered * rescale
    return (normed * gain.astype(jnp.float32) + shift.astype(jnp.float32), normed, rescale)


def norm_back(gradient, normed, rescale, gain):
    scaled = gradient * gain.astype(jnp.float32)
    inner_mean = jnp.mean(scaled * normed, axis=-1, keepdims=True)
    rows_grad = rescale * (scaled - jnp.mean(scaled, axis=-1, keepdims=True) - normed * inner_mean)
    return (rows_grad, jnp.sum(gradient * normed, axis=0), jnp.sum(gradient, axis=0))


def linear(rows, weight, bias):
    return jnp.dot(rows, weight, preferred_element_type=jnp.float32) + bias.astype(jnp.float32)


def weight_grad(rows, gradient):
    return jnp.einsum("ti,to->io", rows, gradient, preferred_element_type=jnp.float32)


def bias_grad(gradient):
    return jnp.sum(gradient.astype(jnp.float32), axis=0)


def back_rows(gradient, weight):
    return jnp.einsum("to,io->ti", gradient, weight, preferred_element_type=jnp.float32)


def gelu_slope(inner):
    normal_cdf = 0.5 * (1.0 + lax.erf(inner * 0.7071067811865476))
    density = jnp.exp(-0.5 * inner * inner) * 0.3989422804014327
    return normal_cdf + inner * density


def masked_scores(queries, key_rows, fragment):
    scaling = queries.shape[-1] ** (-0.5)
    scores = (
        jnp.einsum("qhd,khd->hqk", queries, key_rows, preferred_element_type=jnp.float32) * scaling
    )
    same_fragment = fragment[:, None] == fragment[None, :]
    return jnp.where(same_fragment[None, :, :], scores, -1000000000.0)


def attend_forward(bundle):
    queries, key_rows, value_rows, fragment = bundle
    scores = masked_scores(queries, key_rows, fragment)
    highest = jnp.max(scores, axis=-1, keepdims=True)
    lifted = jnp.exp(scores - highest)
    totals = jnp.sum(lifted, axis=-1, keepdims=True)
    weights = (lifted / totals).astype(jnp.bfloat16)
    mixed = jnp.einsum("hqk,khd->qhd", weights, value_rows, preferred_element_type=jnp.float32)
    return (mixed.astype(jnp.bfloat16), highest + jnp.log(totals))


def attend_backward(bundle):
    queries, key_rows, value_rows, fragment, mixed_grad, log_totals = bundle
    scaling = queries.shape[-1] ** (-0.5)
    weights = jnp.exp(masked_scores(queries, key_rows, fragment) - log_totals)
    value_grad = jnp.einsum(
        "hqk,qhd->khd", weights.astype(jnp.bfloat16), mixed_grad, preferred_element_type=jnp.float32
    )
    prob_grad = jnp.einsum(
        "qhd,khd->hqk", mixed_grad, value_rows, preferred_element_type=jnp.float32
    )
    score_grad = (
        weights * (prob_grad - jnp.sum(prob_grad * weights, axis=-1, keepdims=True))
    ).astype(jnp.bfloat16)
    query_grad = (
        jnp.einsum("hqk,khd->qhd", score_grad, key_rows, preferred_element_type=jnp.float32)
        * scaling
    )
    key_grad = (
        jnp.einsum("hqk,qhd->khd", score_grad, queries, preferred_element_type=jnp.float32)
        * scaling
    )
    return (
        query_grad.astype(jnp.bfloat16),
        key_grad.astype(jnp.bfloat16),
        value_grad.astype(jnp.bfloat16),
    )


def on_device(
    tokens,
    segment_ids,
    query_weight,
    query_bias,
    key_weight,
    value_weight,
    value_bias,
    out_weight,
    out_bias,
    first_gain,
    first_shift,
    expand_weight,
    expand_bias,
    reduce_weight,
    reduce_bias,
    second_gain,
    second_shift,
    cotangent,
):
    seq_count, seq_length = segment_ids.shape
    shaped = (seq_count, seq_length, HEADS, HEAD)
    rows, width = query_weight.shape
    small = (query_bias, value_bias, out_bias, first_gain, first_shift, reduce_bias, second_gain, second_shift)
    small_pack = jnp.concatenate([v[None, :] for v in small] + [expand_bias.reshape(-1, rows)], axis=0)
    gathered_small = lax.all_gather(small_pack, "fsdp", axis=1, tiled=True)
    groups = gathered_small.shape[1] // rows
    vectors = [gathered_small[k] for k in range(8)]
    expand_bias_all = (
        gathered_small[8:].reshape(-1, groups, rows).transpose(1, 0, 2).reshape(groups * expand_bias.shape[0])
    )
    query_bias_all, value_bias_all, out_bias_all, gain1, shift1, reduce_bias_all, gain2, shift2 = vectors
    attention_pack = jnp.stack([query_weight, key_weight, value_weight, out_weight])
    attention_all = lax.all_gather(attention_pack, "fsdp", axis=1, tiled=True)
    expand_all = lax.all_gather(expand_weight, "fsdp", axis=0, tiled=True)
    reduce_all = lax.all_gather(reduce_weight, "fsdp", axis=0, tiled=True)
    wq, wk, wv, wo = attention_all[0], attention_all[1], attention_all[2], attention_all[3]

    queries = linear(tokens, wq, query_bias_all).astype(jnp.bfloat16).reshape(shaped)
    key_rows = jnp.dot(tokens, wk, preferred_element_type=jnp.float32).astype(jnp.bfloat16).reshape(shaped)
    value_rows = linear(tokens, wv, value_bias_all).astype(jnp.bfloat16).reshape(shaped)
    mixed, log_totals = lax.map(attend_forward, (queries, key_rows, value_rows, segment_ids))
    mixed = mixed.reshape(tokens.shape)
    first_sum = tokens.astype(jnp.float32) + linear(mixed, wo, out_bias_all)
    hidden, first_normed, first_rescale = layer_norm(first_sum, gain1, shift1)
    hidden_low = hidden.astype(jnp.bfloat16)
    inner = linear(hidden_low, expand_all, expand_bias_all)
    active = jax.nn.gelu(inner, approximate=False).astype(jnp.bfloat16)
    second_sum = hidden + linear(active, reduce_all, reduce_bias_all)
    output, second_normed, second_rescale = layer_norm(second_sum, gain2, shift2)
    second_grad, grad_second_gain, grad_second_shift = norm_back(
        cotangent.astype(jnp.float32), second_normed, second_rescale, gain2
    )
    branch_grad = second_grad.astype(jnp.bfloat16)
    grad_reduce = weight_grad(active, branch_grad)
    grad_reduce_bias = bias_grad(branch_grad)
    inner_grad = (back_rows(branch_grad, reduce_all) * gelu_slope(inner)).astype(jnp.bfloat16)
    grad_expand = weight_grad(hidden_low, inner_grad)
    grad_expand_bias = bias_grad(inner_grad)
    hidden_grad = second_grad + back_rows(inner_grad, expand_all)
    low = jnp.bfloat16
    scattered_expand = lax.psum_scatter(grad_expand.astype(low), "fsdp", scatter_dimension=0, tiled=True)
    scattered_reduce = lax.psum_scatter(grad_reduce.astype(low), "fsdp", scatter_dimension=0, tiled=True)
    first_grad, grad_first_gain, grad_first_shift = norm_back(
        hidden_grad, first_normed, first_rescale, gain1
    )
    out_grad = first_grad.astype(jnp.bfloat16)
    grad_out = weight_grad(mixed, out_grad)
    grad_out_bias = bias_grad(out_grad)
    mixed_grad = back_rows(out_grad, wo).astype(jnp.bfloat16).reshape(shaped)
    query_grad, key_grad, value_grad = lax.map(
        attend_backward, (queries, key_rows, value_rows, segment_ids, mixed_grad, log_totals)
    )
    query_grad = query_grad.reshape(tokens.shape)
    key_grad = key_grad.reshape(tokens.shape)
    value_grad = value_grad.reshape(tokens.shape)
    grad_query = weight_grad(tokens, query_grad)
    grad_query_bias = bias_grad(query_grad)
    grad_key = weight_grad(tokens, key_grad)
    grad_value = weight_grad(tokens, value_grad)
    grad_value_bias = bias_grad(value_grad)
    input_grad = first_grad + back_rows(query_grad, wq) + back_rows(key_grad, wk) + back_rows(value_grad, wv)
    small_grads = (
        grad_query_bias, grad_value_bias, grad_out_bias, grad_first_gain, grad_first_shift,
        grad_reduce_bias, grad_second_gain, grad_second_shift,
    )
    small_sum = jnp.concatenate(
        [v[None, :] for v in small_grads]
        + [grad_expand_bias.reshape(groups, -1, rows).transpose(1, 0, 2).reshape(-1, groups * rows)],
        axis=0,
    )
    small_sum = lax.psum(small_sum, ("dp", "fsdp"))
    at = lax.axis_index("fsdp") * rows
    small_own = lax.dynamic_slice_in_dim(small_sum, at, rows, axis=1)
    attention_grads = jnp.concatenate([grad_query, grad_key, grad_value, grad_out], axis=1).astype(low)
    attention_own = lax.psum_scatter(attention_grads, "fsdp", scatter_dimension=0, tiled=True)
    attention_own = lax.psum(attention_own, "dp").astype(jnp.float32)
    attention_own = [attention_own[:, k * width : (k + 1) * width] for k in range(4)]
    expand_own = lax.psum(scattered_expand, "dp").astype(jnp.float32)
    reduce_own = lax.psum(scattered_reduce, "dp").astype(jnp.float32)
    return (
        output.astype(jnp.bfloat16),
        input_grad,
        attention_own[0],
        small_own[0],
        attention_own[1],
        attention_own[2],
        small_own[1],
        attention_own[3],
        small_own[2],
        small_own[3],
        small_own[4],
        expand_own,
        small_own[8:].reshape(-1),
        reduce_own,
        small_own[5],
        small_own[6],
        small_own[7],
    )


def solution(mesh):
    in_specs = (
        P(("dp", "fsdp"), None),
        P(("dp", "fsdp"), None),
        P("fsdp", None),
        P("fsdp"),
        P("fsdp", None),
        P("fsdp", None),
        P("fsdp"),
        P("fsdp", None),
        P("fsdp"),
        P("fsdp"),
        P("fsdp"),
        P("fsdp", None),
        P("fsdp"),
        P("fsdp", None),
        P("fsdp"),
        P("fsdp"),
        P("fsdp"),
        P(("dp", "fsdp"), None),
    )
    out_specs = (
        P(("dp", "fsdp"), None),
        P(("dp", "fsdp"), None),
        P("fsdp", None),
        P("fsdp"),
        P("fsdp", None),
        P("fsdp", None),
        P("fsdp"),
        P("fsdp", None),
        P("fsdp"),
        P("fsdp"),
        P("fsdp"),
        P("fsdp", None),
        P("fsdp"),
        P("fsdp", None),
        P("fsdp"),
        P("fsdp"),
        P("fsdp"),
    )
    return jax.shard_map(
        on_device, mesh=mesh, in_specs=in_specs, out_specs=out_specs, check_vma=False
    )
```

time: 995 us -> 755 us (0.76)
  waiting for transfers between devices: 553 us -> 381 us
  blocking collectives: 90.7 us -> 62.2 us
  matrix products: 195 us -> 177 us
  local copies, waits for them, and re-layouts: 85.1 us -> 70.2 us
    reduce_scatter x3 -> x2, waiting for transfers between devices: 265 us -> 195 us  [the longest x1 98.9 us: on_device(): lax.psum_scatter(grad_expand.astype(low), 'fsdp', scatter_dimension=0, ti...]
    unnamed x2 -> x0, blocking collectives: 55.3 us -> none
    all_gather x6 -> x3, waiting for transfers between devices: 154 us -> 118 us  [the longest x1 49.7 us: on_device(): attention_all = lax.all_gather(attention_pack, 'fsdp', axis=1, tiled=True)]
    psum x1, waiting for transfers between devices: 36.3 us -> 0.01 us  [on_device(): attention_own = lax.psum(attention_own, 'dp').astype(jnp.float32)]
    unnamed x16 -> x8, waiting for transfers between devices: 97.4 us -> 67.4 us
    psum x1, blocking collectives: 13 us -> 39.5 us  [on_device(): small_sum = lax.psum(small_sum, ('dp', 'fsdp'))]
    unnamed x156 -> x99, local copies, waits for them, and re-layouts: 48.2 us -> 27.3 us
    dot_general x5, matrix products: 70.2 us -> 58.6 us  [linear(): jnp.dot(rows, weight, preferred_element_type=jnp.float32)]
  transfers between devices with their start and end apart: 13 -> 7, of which waited for: 11 -> 6; matrix products, arithmetic and copies ran while one was open for 19% -> 19% of each run, Pallas kernels for 0% -> 0%
where the time goes in v1:
time: 755 us; the launch traced here: 744 us
  waiting for transfers between devices  381 us (50%)
  matrix products  177 us (23%)
  local copies, waits for them, and re-layouts  70.2 us (9%)
  blocking collectives  62.2 us (8%)
  other arithmetic  37.5 us (5%)
  between operations  15 us (2%)
    reduce_scatter x1, waiting for transfers between devices, on_device(): lax.psum_scatter(grad_expand.astype(low), 'fsdp', scatter_dimension=0, ti...  98.9 us
    reduce_scatter x1, waiting for transfers between devices, on_device(): lax.psum_scatter(grad_reduce.astype(low), 'fsdp', scatter_dimension=0, ti...  96.6 us
    unnamed x8, waiting for transfers between devices  67.4 us
    dot_general x5, matrix products, linear(): jnp.dot(rows, weight, preferred_element_type=jnp.float32)  58.6 us
    all_gather x1, waiting for transfers between devices, on_device(): attention_all = lax.all_gather(attention_pack, 'fsdp', axis=1, tiled=True)  49.7 us
    dot_general x6, matrix products, back_rows(): jnp.einsum('to,io->ti', gradient, weight, preferred_element_type=jnp.floa...  43.4 us
    all_gather x1, waiting for transfers between devices, on_device(): reduce_all = lax.all_gather(reduce_weight, 'fsdp', axis=0, tiled=True)  41 us
    psum x1, blocking collectives, on_device(): small_sum = lax.psum(small_sum, ('dp', 'fsdp'))  39.5 us
  transfers between devices with their start and end apart: 7, of which 6 were waited for; matrix products, arithmetic and copies ran while one was open for 19% of the time, Pallas kernels for 0%

profile of v1, /device:TPU:11, one launch (start us, length us, event | category | flops | bytes accessed | tf_op | source)
XLA Modules:
  0.0 744.1 jit_solution(9849128868682423253)
XLA Ops:
  12.6 22.7 %all-gather = bf16[8,96,12]{1,2,0:T(8,128)(2,1)S(1)} all-gather(bf16[1,96,12]{1,2,0:T(8,128)(2,1)S(1)} %bitcast.250), channel_id=1, replica_groups=mesh['dp'=4,'fsdp'=8] {'fsdp'}, dimensions={0}, use_global_device_ids=true | all-gather | bytes 20736 | tf_op jit(solution)/shard_map/all_gather | solution.py:120
  39.4 49.7 %all-gather.5.cloned.1.call-done = bf16[4,768,768]{2,1,0:T(8,128)(2,1)} async-done(((bf16[4,96,768]{2,1,0:T(8,128)(2,1)}), bf16[4,768,768]{2,1,0:T(8,128)(2,1)}) %all-gather.5.cloned.1.call-update) | async-done | bytes 4718608 | tf_op jit(solution)/shard_map/all_gather | solution.py:128
  111.6 21.0 %while.26 = (s32[]{:T(128)}, bf16[2,512,12,64]{1,3,2,0:T(8,128)(2,1)}, f32[2,12,512,1]{2,1,3,0:T(8,128)S(1)}, bf16[2,512,12,64]{1,3,2,0:T(8,128)(2,1)}, s32[2,51...) while((s32[]{:T(128)}, ...), condition=%wide.region_3.4_spmd, body=%wide.region_0.3_spmd.sunk | while | flops 843704320 | bytes 42172516 | solution.py:136
  116.7 5.5 fusion.152
  127.0 5.5 fusion.152
  141.8 27.2 %all-gather.7.cloned.1.call-done = bf16[768,3072]{1,0:T(8,128)(2,1)} async-done(((bf16[96,3072]{1,0:T(8,128)(2,1)}), bf16[768,3072]{1,0:T(8,128)(2,1)}) %all-gather.7.cloned.1.call-update) | async-done | bytes 4718608 | tf_op jit(solution)/shard_map/all_gather | solution.py:129
  169.0 39.0 %fusion.59 = (bf16[1024,3072]{1,0:T(8,128)(2,1)}, f32[1024,3072]{1,0:T(8,128)}) fusion(f32[3072]{0:T(1024)S(1)} %reshape.228, bf16[768,3072]{1,0:T(8,128)(2,1)} %all-gather.7.cloned.1.call-done, f32[1024,768]{0,1:T(8,128)} %copy-done.6, f32[768]{0:T(1024)S(1)} %get-tuple-element.261, f32[768]{0:T(1024)S(1)} %get-tuple-element.262, ...), kind=kOutput, calls=%fused_computation.68 | convolution fusion | flops 5043388416 | bytes 26765312 | tf_op jit(solution)/shard_map/dot_general | solution.py:26
  208.0 41.0 %all-gather.9.cloned.1.call-done = bf16[3072,768]{1,0:T(8,128)(2,1)} async-done(((bf16[384,768]{1,0:T(8,128)(2,1)}), bf16[3072,768]{1,0:T(8,128)(2,1)}) %all-gather.9.cloned.1.call-update) | async-done | bytes 4718608 | tf_op jit(solution)/shard_map/all_gather | solution.py:130
  248.9 9.4 %fusion.106 = (f32[1024]{0:T(1024)S(1)}, f32[1024,768]{0,1:T(8,128)S(1)}) fusion(f32[768]{0:T(1024)S(1)} %copy-done.42, bf16[1024,3072]{1,0:T(8,128)(2,1)} %get-tuple-element.326, bf16[3072,768]{1,0:T(8,128)(2,1)} %all-gather.9.cloned.1.call-done, f32[768]{0:T(1024)S(1)} %get-tuple-element.261, f32[768]{0:T(1024)S(1)} %get-tuple-element.262, ...), kind=kOutput, calls=%fused_computation.184 | convolution fusion | flops 4837342208 | bytes 17323008 | tf_op jit(solution)/shard_map/dot_general | solution.py:26
  265.0 14.7 %convert_reduce_fusion = (f32[3072]{0:T(1024)}, bf16[1024,3072]{1,0:T(8,128)(2,1)}) fusion(f32[1024,3072]{1,0:T(8,128)} %get-tuple-element.327, f32[3072]{0:T(1024)S(1)} %reshape.228, bf16[1024,768]{0,1:T(8,128)(2,1)S(1)} %get-tuple-element.304, bf16[3072,768]{1,0:T(8,128)(2,1)S(1)} %copy-done.45), kind=kOutput, calls=%fused_computation.75 | convolution fusion | flops 4872729600 | bytes 25190400 | tf_op jit(solution)/shard_map/to,io->ti/dot_general | solution.py:38
  279.8 9.9 %multiply_reduce_fusion.1 = (f32[768]{0:T(1024)}, f32[1024]{0:T(1024)S(1)}, f32[1024]{0:T(1024)S(1)}, f32[768]{0:T(1024)}, f32[1024,768]{0,1:T(8,128)S(1)}) fusion(f32[1024,768]{0,1:T(8,128)S(1)} %copy-done.7, f32[1024]{0:T(1024)S(1)} %add_rsqrt_fusion.1, f32[1024]{0:T(1024)S(1)} %broadcast_multiply_fusion.5, f32[768]{0:T(1024)S(1)} %get-tuple-element.262, ...), kind=kOutput, calls=%fused_computation.105 | convolution fusion | flops 4845989888 | bytes 22065152 | tf_op jit(solution)/shard_map/to,io->ti/dot_general | solution.py:38
  311.1 49.2 %while.27 = (s32[]{:T(128)}, bf16[2,512,12,64]{1,3,2,0:T(8,128)(2,1)}, bf16[2,512,12,64]{1,3,2,0:T(8,128)(2,1)}, bf16[2,512,12,64]{1,3,2,0:T(8,128)(2,1)}, bf16[...) while((s32[]{:T(128)}, ...), condition=%wide.region_14.15_spmd, body=%wide.region_12.14_spmd.sunk | while | flops 2062673920 | bytes 141233456 | solution.py:165
  317.2 6.9 multiply_reduce_fusion.7
  324.0 7.1 multiply_convert_fusion.4
  341.6 6.9 multiply_reduce_fusion.7
  348.5 7.1 multiply_convert_fusion.4
  376.2 6.6 copy.162
  382.9 9.4 %convolution_convert_fusion = bf16[3072,768]{1,0:T(8,128)(2,1)} fusion(bf16[1024,3072]{1,0:T(8,128)(2,1)} %get-tuple-element.326, bf16[1024,768]{0,1:T(8,128)(2,1)} %copy-done.22), kind=kOutput, calls=%fused_computation.91 | convolution fusion | flops 4834197504 | bytes 12582912 | tf_op jit(solution)/shard_map/ti,to->io/dot_general | solution.py:30
  393.0 9.9 %convolution_convert_fusion.1 = bf16[768,3072]{1,0:T(8,128)(2,1)} fusion(bf16[1024,3072]{1,0:T(8,128)(2,1)} %get-tuple-element.332, f32[1024,768]{0,1:T(8,128)} %copy-done.6, f32[768]{0:T(1024)S(1)} %copy-done.41, f32[768]{0:T(1024)S(1)} %copy-done.31, f32[1024]{0:T(1024)S(1)} %copy-done.36, f32[1024]{0:T(1024)S(1)} %copy-done.28), kind=kOutput, calls=%fused_computation.92 | convolution fusion | flops 4838129664 | bytes 14170112 | tf_op jit(solution)/shard_map/ti,to->io/dot_general | solution.py:30
  413.5 66.0 %reduce-scatter.10.cloned.1.call-done = bf16[96,3072]{1,0:T(8,128)(2,1)} async-done(((bf16[768,3072]{1,0:T(8,128)(2,1)}), bf16[96,3072]{1,0:T(8,128)(2,1)}) %reduce-scatter.10.cloned.1.call-update) | async-done | bytes 589840
  481.7 96.6 %reduce-scatter.8.cloned.1.call-done = bf16[384,768]{1,0:T(8,128)(2,1)} async-done(((bf16[3072,768]{1,0:T(8,128)(2,1)}), bf16[384,768]{1,0:T(8,128)(2,1)}) %reduce-scatter.8.cloned.1.call-update) | async-done | bytes 589840 | tf_op jit(solution)/shard_map/reduce_scatter | solution.py:157
  578.3 98.9 %reduce-scatter.6.cloned.1.call-done = bf16[96,3072]{1,0:T(8,128)(2,1)} async-done(((bf16[768,3072]{1,0:T(8,128)(2,1)}), bf16[96,3072]{1,0:T(8,128)(2,1)}) %reduce-scatter.6.cloned.1.call-update) | async-done | bytes 589840 | tf_op jit(solution)/shard_map/reduce_scatter | solution.py:156
  678.0 39.5 %psum.29 = f32[12,768]{1,0:T(8,128)S(1)} all-reduce(f32[12,768]{1,0:T(8,128)S(1)} %concatenate.12), channel_id=1, replica_groups=mesh['dp'=4,'fsdp'=8] {'dp','fsdp'}, use_global_device_ids=true, to_apply=%region_26.27 | all-reduce | flops 9216 | bytes 73728 | tf_op jit(solution)/shard_map/psum | solution.py:186
  718.3 6.1 add_add_fusion
  (233 shorter events, 143.0 us)
Async XLA Ops:
  7.2 29.0 %copy-start.12 = (bf16[1024,768]{1,0:T(8,128)(2,1)S(1)}, bf16[1024,768]{1,0:T(8,128)(2,1)}, u32[]{:S(2)}) copy-start(bf16[1024,768]{1,0:T(8,128)(2,1)} %param.39) | copy-start | bytes 4718596
  7.2 81.9 %all-gather.5.cloned.1.call-start = ((), (), s32[]{:S(2)}) async-start(), calls=%async_computation.3 | async-start | bytes 5308416 | tf_op jit(solution)/shard_map/all_gather | solution.py:128
  7.2 30.6 %copy-start.13 = (bf16[1024,768]{1,0:T(8,128)(2,1)S(1)}, bf16[1024,768]{1,0:T(8,128)(2,1)}, u32[]{:S(2)}) copy-start(bf16[1024,768]{1,0:T(8,128)(2,1)} %param.22) | copy-start | bytes 4718596
  9.4 159.5 %all-gather.7.cloned.1.call-start = ((), (), s32[]{:S(2)}) async-start(), calls=%async_computation.4 | async-start | bytes 5308416 | tf_op jit(solution)/shard_map/all_gather | solution.py:129
  10.2 238.7 %all-gather.9.cloned.1.call-start = ((), (), s32[]{:S(2)}) async-start(), calls=%async_computation.5 | async-start | bytes 5308416 | tf_op jit(solution)/shard_map/all_gather | solution.py:130
  10.9 468.6 %reduce-scatter.10.cloned.1.call-start = ((), (), s32[]{:S(2)}) async-start(), calls=%async_computation.8 | async-start | bytes 5308416
  36.0 212.9 %copy-start.40 = (f32[768]{0:T(1024)}, f32[768]{0:T(1024)S(1)}, u32[]{:S(2)}) copy-start(f32[768]{0:T(1024)S(1)} %get-tuple-element.261) | copy-start | bytes 9220
  36.0 253.6 %copy-start.30 = (f32[768]{0:T(1024)}, f32[768]{0:T(1024)S(1)}, u32[]{:S(2)}) copy-start(f32[768]{0:T(1024)S(1)} %get-tuple-element.262) | copy-start | bytes 9220
  139.7 149.9 %copy-start.27 = (f32[1024]{0:T(1024)}, f32[1024]{0:T(1024)S(1)}, u32[]{:S(2)}) copy-start(f32[1024]{0:T(1024)S(1)} %broadcast_multiply_fusion.5) | copy-start | bytes 12292
  141.8 147.9 %copy-start.35 = (f32[1024]{0:T(1024)}, f32[1024]{0:T(1024)S(1)}, u32[]{:S(2)}) copy-start(f32[1024]{0:T(1024)S(1)} %add_rsqrt_fusion.1) | copy-start | bytes 12292
  169.0 79.9 %copy-start.42 = (f32[768]{0:T(1024)S(1)}, f32[768]{0:T(1024)}, u32[]{:S(2)}) copy-start(f32[768]{0:T(1024)} %get-tuple-element.260) | copy-start | bytes 9220
  261.8 18.0 %slice-start = ((s8[4718592]{0:T(1024)(128)(4,1)}), s8[4194304]{0:T(1024)(128)(4,1)S(1)}, s32[]{:S(2)}) async-start(s8[4718592]{0:T(1024)(128)(4,1)} %bitcast.259), calls=%async_computation.10 | async-start | bytes 8388608
  265.0 14.7 %copy-start.7 = (f32[1024,768]{0,1:T(8,128)S(1)}, f32[1024,768]{0,1:T(8,128)}, u32[]{:S(2)}) copy-start(f32[1024,768]{0,1:T(8,128)} %copy-done.6) | copy-start | bytes 9437188
  265.0 14.7 %slice-start.1 = ((s8[4718592]{0:T(1024)(128)(4,1)}), s8[524288]{0:T(1024)(128)(4,1)S(1)}, s32[]{:S(2)}) async-start(s8[4718592]{0:T(1024)(128)(4,1)} %bitcast.259), calls=%async_computation.11 | async-start | bytes 1048576
  382.8 195.5 %reduce-scatter.8.cloned.1.call-start = ((), (), s32[]{:S(2)}) async-start(), calls=%async_computation.7 | async-start | bytes 5308416 | tf_op jit(solution)/shard_map/reduce_scatter | solution.py:157
  392.3 284.8 %reduce-scatter.6.cloned.1.call-start = ((), (), s32[]{:S(2)}) async-start(), calls=%async_computation.6 | async-start | bytes 5308416 | tf_op jit(solution)/shard_map/reduce_scatter | solution.py:156
  402.9 327.0 %all-reduce.3.cloned.1.call-start = ((), (), s32[]{:S(2)}) async-start(), calls=%async_computation.9 | async-start | bytes 3932160 | tf_op jit(solution)/shard_map/psum | solution.py:191
  413.5 264.0 %copy-start.38 = (f32[768]{0:T(1024)S(1)}, f32[768]{0:T(1024)}, u32[]{:S(2)}) copy-start(f32[768]{0:T(1024)} %get-tuple-element.252) | copy-start | bytes 9220
  413.5 264.0 %copy-start.37 = (f32[768]{0:T(1024)S(1)}, f32[768]{0:T(1024)}, u32[]{:S(2)}) copy-start(f32[768]{0:T(1024)} %get-tuple-element.257) | copy-start | bytes 9220
  413.5 264.0 %copy-start.44 = (f32[768]{0:T(1024)S(1)}, f32[768]{0:T(1024)}, u32[]{:S(2)}) copy-start(f32[768]{0:T(1024)} %get-tuple-element.250) | copy-start | bytes 9220
  413.5 264.1 %copy-start.33 = (f32[768]{0:T(1024)S(1)}, f32[768]{0:T(1024)}, u32[]{:S(2)}) copy-start(f32[768]{0:T(1024)} %get-tuple-element.303) | copy-start | bytes 9220
  413.5 264.1 %copy-start.43 = (f32[768]{0:T(1024)S(1)}, f32[768]{0:T(1024)}, u32[]{:S(2)}) copy-start(f32[768]{0:T(1024)} %get-tuple-element.255) | copy-start | bytes 9220
  413.5 264.1 %copy-start.34 = (f32[768]{0:T(1024)S(1)}, f32[768]{0:T(1024)}, u32[]{:S(2)}) copy-start(f32[768]{0:T(1024)} %get-tuple-element.305) | copy-start | bytes 9220
  413.5 264.1 %copy-start.39 = (f32[3072]{0:T(1024)S(1)}, f32[3072]{0:T(1024)}, u32[]{:S(2)}) copy-start(f32[3072]{0:T(1024)} %get-tuple-element.331) | copy-start | bytes 36868
  (37 other events, 110.2 us)
Sparse Core Ops, SparseCore 0:
  10.8 78.2 all-gather.4
  91.3 77.6 all-gather.6
  171.2 77.6 all-gather.8
  383.0 96.4 reduce-scatter.9
  483.0 95.2 reduce-scatter.7
  581.8 95.3 reduce-scatter.5
  680.3 49.1 all-reduce.2

commit v2 on v1

--- a/solution.py
+++ b/solution.py
@@ -1,10 +1,15 @@
+import functools
+
 import jax
 import jax.numpy as jnp
 from jax import lax
+from jax.experimental import pallas as pl
+from jax.experimental.pallas import tpu as pltpu
 from jax.sharding import PartitionSpec as P
 
 HEADS = 12
 HEAD = 64
+SMALL = 32
 
 
 def layer_norm(rows, gain, shift):
@@ -92,7 +97,355 @@
     )
 
 
-def on_device(
+MESH = pl.DeviceIdType.MESH
+LINE = 4
+ORDER = (3, 0, 2, 1)
+
+
+def places():
+    dp, fs = lax.axis_index("dp"), lax.axis_index("fsdp")
+    core, y, z = lax.rem(dp, 2), lax.rem(fs, 2), fs // 2
+    return dict(
+        core=core, y=y, z=z, fs=fs,
+        sibling=(dp + 1 - 2 * core, fs),
+        across=(lax.rem(dp + 2, 4), fs),
+        side=(dp, fs + 1 - 2 * y),
+        up=(dp, fs + 2),
+        down=(dp, fs - 2),
+    )
+
+
+def greet(at):
+    barrier = pltpu.get_barrier_semaphore()
+
+    def hello(who):
+        pl.semaphore_signal(barrier, inc=1, device_id=who, device_id_type=MESH)
+
+    for name in ("sibling", "across", "side"):
+        hello(at[name])
+    pl.when(at["z"] < LINE - 1)(lambda: hello(at["up"]))
+    pl.when(at["z"] > 0)(lambda: hello(at["down"]))
+    end = jnp.logical_or(at["z"] == 0, at["z"] == LINE - 1)
+    pl.when(end)(lambda: pl.semaphore_wait(barrier, 4))
+    pl.when(jnp.logical_not(end))(lambda: pl.semaphore_wait(barrier, 5))
+
+
+def add_rows(target, *sources):
+    rows = target.shape[0]
+
+    def block(k, carry):
+        at = pl.ds(pl.multiple_of(k * 16, 16), 16)
+        total = sources[0][at, :].astype(jnp.float32)
+        for source in sources[1:]:
+            total = total + source[at, :].astype(jnp.float32)
+        target[at, :] = total.astype(jnp.bfloat16)
+        return carry
+
+    lax.fori_loop(0, rows // 16, block, 0)
+
+
+def scatter_scratch(rows, columns):
+    half = rows // 2
+    low = jnp.bfloat16
+    return [
+        pltpu.VMEM((2, LINE, half, columns), low),
+        pltpu.VMEM((2, LINE, half, columns), low),
+        pltpu.VMEM((LINE, half, columns), low),
+        pltpu.VMEM((2, LINE, half, columns), low),
+        pltpu.VMEM((half, columns), low),
+        pltpu.VMEM((2, half, columns), low),
+        pltpu.SemaphoreType.DMA((2,)),
+        pltpu.SemaphoreType.DMA((2, 2)),
+        pltpu.SemaphoreType.DMA((2, LINE)),
+        pltpu.SemaphoreType.DMA((2, 2, LINE)),
+        pltpu.SemaphoreType.DMA((2, 2)),
+    ]
+
+
+SCRATCHES = 11
+
+
+def scatter_events(at, source, out, scratch):
+    own, sib, side, line, across, result, load_sem, sib_sem, side_sem, line_sem, last_sem = scratch
+    half = own.shape[2]
+    core, y, z = at["core"], at["y"], at["z"]
+    mine = pl.ds(pl.multiple_of(core * half, 16), half)
+    other = pl.ds(pl.multiple_of((1 - core) * half, 16), half)
+    column = (1 - y, y)
+
+    def load(k):
+        return pltpu.make_async_copy(source.at[:, column[k], mine, :], own.at[k], load_sem.at[k])
+
+    def remote(src, dst, send, recv, who):
+        return pltpu.make_async_remote_copy(
+            src_ref=src, dst_ref=dst, send_sem=send, recv_sem=recv, device_id=at[who], device_id_type=MESH
+        )
+
+    def to_sibling(k):
+        return remote(source.at[:, column[k], other, :], sib.at[k], sib_sem.at[0, k], sib_sem.at[1, k], "sibling")
+
+    def to_side(k):
+        return remote(own.at[0, k], side.at[k], side_sem.at[0, k], side_sem.at[1, k], "side")
+
+    def to_line(way, k):
+        return remote(
+            own.at[1, k], line.at[way, k], line_sem.at[0, way, k], line_sem.at[1, way, k], ("up", "down")[way]
+        )
+
+    def to_across():
+        return remote(own.at[1, z], across, last_sem.at[0, 0], last_sem.at[1, 0], "across")
+
+    def to_last():
+        return remote(result.at[core], result.at[core], last_sem.at[0, 1], last_sem.at[1, 1], "sibling")
+
+    def begin():
+        for k in range(2):
+            to_sibling(k).start()
+            load(k).start()
+
+    def first():
+        load(0).wait()
+        to_sibling(0).wait_recv()
+        for k in ORDER:
+            add_rows(own.at[0, k], own.at[0, k], sib.at[0, k])
+            to_side(k).start()
+        load(1).wait()
+        to_sibling(1).wait_recv()
+        for k in ORDER:
+            add_rows(own.at[1, k], own.at[1, k], sib.at[1, k])
+
+    def chain(k):
+        to_side(k).wait_recv()
+
+        def pass_on(way, inner):
+            @pl.when(inner)
+            def _():
+                to_line(way, k).wait_recv()
+                add_rows(own.at[1, k], own.at[1, k], side.at[k], line.at[way, k])
+
+            @pl.when(jnp.logical_not(inner))
+            def _():
+                add_rows(own.at[1, k], own.at[1, k], side.at[k])
+
+            to_line(way, k).start()
+
+        pl.when(k > z)(lambda: pass_on(0, z > 0))
+        pl.when(k < z)(lambda: pass_on(1, z < LINE - 1))
+        pl.when(k == z)(lambda: add_rows(own.at[1, k], own.at[1, k], side.at[k]))
+
+    def gather_line():
+        for k in range(LINE):
+
+            @pl.when(k == z)
+            def _():
+                parts = []
+                if k > 0:
+                    to_line(0, k).wait_recv()
+                    parts.append(line.at[0, k])
+                if k < LINE - 1:
+                    to_line(1, k).wait_recv()
+                    parts.append(line.at[1, k])
+                add_rows(own.at[1, k], own.at[1, k], *parts)
+
+        to_across().start()
+
+    def finish():
+        to_across().wait_recv()
+        add_rows(result.at[core], own.at[1, z], across)
+        to_last().start()
+
+    def drain():
+        to_last().wait_recv()
+        out[0:half, :] = result[0]
+        out[half : 2 * half, :] = result[1]
+        to_last().wait_send()
+        to_across().wait_send()
+        for k in range(2):
+            to_sibling(k).wait_send()
+        for k in range(LINE):
+            to_side(k).wait_send()
+            pl.when(k > z)(lambda: to_line(0, k).wait_send())
+            pl.when(k < z)(lambda: to_line(1, k).wait_send())
+
+    chains = [functools.partial(chain, k) for k in ORDER]
+    return begin, first, chains, gather_line, finish, drain
+
+
+def scatter_kernel(count, *refs):
+    sources, outs, scratch = refs[:count], refs[count : 2 * count], refs[2 * count :]
+    at = places()
+    greet(at)
+    parts = [
+        scatter_events(at, sources[g], outs[g], scratch[g * SCRATCHES : (g + 1) * SCRATCHES]) for g in range(count)
+    ]
+    for begin, *_ in parts:
+        begin()
+    for _, first, *_ in parts:
+        first()
+    for _, _, chains, *_ in parts:
+        for step in chains:
+            step()
+    for part in parts:
+        part[3]()
+    for part in parts:
+        part[4]()
+    for part in parts:
+        part[5]()
+
+
+def scatter_all(sources, ident):
+    shapes = [s.shape[2:] for s in sources]
+    return pl.pallas_call(
+        functools.partial(scatter_kernel, len(sources)),
+        out_shape=[jax.ShapeDtypeStruct(s, jnp.bfloat16) for s in shapes],
+        in_specs=[pl.BlockSpec(memory_space=pl.ANY)] * len(sources),
+        out_specs=[pl.BlockSpec(memory_space=pltpu.VMEM)] * len(sources),
+        scratch_shapes=[x for s in shapes for x in scatter_scratch(*s)],
+        compiler_params=pltpu.CompilerParams(
+            collective_id=ident, has_side_effects=True, vmem_limit_bytes=60 * 1024 * 1024
+        ),
+        name="scatter_sum",
+    )(*sources)
+
+
+def gather_scratch():
+    return [pltpu.SemaphoreType.DMA((2 * LINE, 2)), pltpu.SemaphoreType.DMA((2 * LINE, 4))]
+
+
+def gather_events(at, shard, whole, scratch):
+    arrived, sent = scratch
+    half = shard.shape[0] // 2
+    core, y, z, me = at["core"], at["y"], at["z"], at["fs"]
+    mine = pl.ds(pl.multiple_of(core * half, 16), half)
+    ways = ("side", "up", "down")
+
+    def pass_on(src, owner, way):
+        return pltpu.make_async_remote_copy(
+            src_ref=src,
+            dst_ref=whole.at[owner, mine, :],
+            send_sem=sent.at[owner, way],
+            recv_sem=arrived.at[owner, core],
+            device_id=at[ways[way]],
+            device_id_type=MESH,
+        )
+
+    def half_to_sibling(owner):
+        return pltpu.make_async_remote_copy(
+            src_ref=whole.at[owner, mine, :],
+            dst_ref=whole.at[owner, mine, :],
+            send_sem=sent.at[owner, 3],
+            recv_sem=arrived.at[owner, core],
+            device_id=at["sibling"],
+            device_id_type=MESH,
+        )
+
+    def half_from_sibling(owner):
+        theirs = pl.ds(pl.multiple_of((1 - core) * half, 16), half)
+        return pltpu.make_async_remote_copy(
+            src_ref=whole.at[owner, theirs, :],
+            dst_ref=whole.at[owner, theirs, :],
+            send_sem=sent.at[owner, 3],
+            recv_sem=arrived.at[owner, 1 - core],
+            device_id=at["sibling"],
+            device_id_type=MESH,
+        )
+
+    def own_to_sibling():
+        return pltpu.make_async_remote_copy(
+            src_ref=shard,
+            dst_ref=whole.at[me],
+            send_sem=sent.at[me, 3],
+            recv_sem=arrived.at[me, 0],
+            device_id=at["sibling"],
+            device_id_type=MESH,
+        )
+
+    def begin():
+        src = shard.at[mine, :]
+        pl.when(z < LINE - 1)(lambda: pass_on(src, me, 1).start())
+        pl.when(z > 0)(lambda: pass_on(src, me, 2).start())
+        pass_on(src, me, 0).start()
+        own_to_sibling().start()
+
+    def relay(t, sign):
+        owner = me + 2 * t * sign
+
+        @pl.when((z - t >= 0) if sign < 0 else (z + t <= LINE - 1))
+        def _():
+            held = whole.at[owner, mine, :]
+            pass_on(held, owner, 0).wait_recv()
+            if sign < 0:
+                pl.when(z < LINE - 1)(lambda: pass_on(held, owner, 1).start())
+            else:
+                pl.when(z > 0)(lambda: pass_on(held, owner, 2).start())
+            pass_on(held, owner, 0).start()
+            half_to_sibling(owner).start()
+
+    def from_side(t, sign):
+        owner = me + 1 - 2 * y + 2 * t * sign
+
+        @pl.when((z - t >= 0) if sign < 0 else (z + t <= LINE - 1))
+        def _():
+            pass_on(whole.at[owner, mine, :], owner, 0).wait_recv()
+            half_to_sibling(owner).start()
+
+    def settle():
+        own_to_sibling().wait_recv()
+        for owner in range(2 * LINE):
+            pl.when(owner != me)(lambda: half_from_sibling(owner).wait_recv())
+
+    def drain():
+        own_to_sibling().wait_send()
+        src = shard.at[mine, :]
+        for owner in range(2 * LINE):
+            line = owner // 2
+            same = owner % 2 == y
+
+            @pl.when(same)
+            def _():
+                pass_on(src, owner, 0).wait_send()
+                pl.when(jnp.logical_and(line <= z, z < LINE - 1))(lambda: pass_on(src, owner, 1).wait_send())
+                pl.when(jnp.logical_and(line >= z, z > 0))(lambda: pass_on(src, owner, 2).wait_send())
+
+            pl.when(owner != me)(lambda: half_to_sibling(owner).wait_send())
+
+    relays = [functools.partial(relay, t, s) for t in range(1, LINE) for s in (-1, 1)]
+    sides = [functools.partial(from_side, 0, 1)]
+    sides += [functools.partial(from_side, t, s) for t in range(1, LINE) for s in (-1, 1)]
+    return begin, relays, sides, settle, drain
+
+
+def gather_kernel(count, *refs):
+    shards, wholes, scratch = refs[:count], refs[count : 2 * count], refs[2 * count :]
+    at = places()
+    greet(at)
+    parts = [gather_events(at, shards[g], wholes[g], scratch[2 * g : 2 * g + 2]) for g in range(count)]
+    for begin, *_ in parts:
+        begin()
+    for _, relays, sides, *_ in parts:
+        for step in relays:
+            step()
+    for _, relays, sides, *_ in parts:
+        for step in sides:
+            step()
+    for part in parts:
+        part[3]()
+        part[4]()
+
+
+def gather_all(shards, ident):
+    return pl.pallas_call(
+        functools.partial(gather_kernel, len(shards)),
+        out_shape=[jax.ShapeDtypeStruct((2 * LINE, *s.shape), jnp.bfloat16) for s in shards],
+        in_specs=[pl.BlockSpec(memory_space=pltpu.VMEM)] * len(shards),
+        out_specs=[pl.BlockSpec(memory_space=pltpu.VMEM)] * len(shards),
+        scratch_shapes=[x for s in shards for x in gather_scratch()],
+        compiler_params=pltpu.CompilerParams(collective_id=ident, has_side_effects=True, vmem_limit_bytes=60 * 1024 * 1024),
+        name="gather",
+    )(*shards)
+
+
+def plain_on_device(
     tokens,
     segment_ids,
     query_weight,
@@ -213,7 +566,141 @@
     )
 
 
+def on_device(
+    tokens,
+    segment_ids,
+    query_weight,
+    query_bias,
+    key_weight,
+    value_weight,
+    value_bias,
+    out_weight,
+    out_bias,
+    first_gain,
+    first_shift,
+    expand_weight,
+    expand_bias,
+    reduce_weight,
+    reduce_bias,
+    second_gain,
+    second_shift,
+    cotangent,
+):
+    seq_count, seq_length = segment_ids.shape
+    shaped = (seq_count, seq_length, HEADS, HEAD)
+    rows, width = query_weight.shape
+    low = jnp.bfloat16
+    me = lax.axis_index("fsdp")
+    shards = 2 * LINE
+    vectors = jnp.stack(
+        [query_bias, value_bias, out_bias, first_gain, first_shift, reduce_bias, second_gain, second_shift]
+    )
+    count = expand_bias.shape[0]
+    per_row = width // count
+    small = lax.dynamic_update_slice(jnp.zeros((SMALL, width), low), vectors, (0, me * rows))
+    small = lax.dynamic_update_slice(small, expand_bias[None, :], (8 + me // per_row, lax.rem(me, per_row) * count))
+    pack = jnp.concatenate([query_weight, key_weight, value_weight, out_weight, small], axis=0)
+    (attention_all,) = gather_all([pack], 0)
+    wq, wk, wv, wo = [attention_all[:, k * rows : (k + 1) * rows].reshape(width, width) for k in range(4)]
+    small_all = jnp.sum(attention_all[:, 4 * rows :].astype(jnp.float32), axis=0)
+    query_bias_all, value_bias_all, out_bias_all, gain1, shift1, reduce_bias_all, gain2, shift2 = [
+        small_all[k] for k in range(8)
+    ]
+    expand_bias_all = small_all[8 : 8 + shards // per_row].reshape(-1)
+    expand_all, reduce_all = gather_all([expand_weight, reduce_weight], 1)
+    expand_all = expand_all.reshape(width, -1)
+    reduce_all = reduce_all.reshape(-1, width)
+
+    queries = linear(tokens, wq, query_bias_all).astype(jnp.bfloat16).reshape(shaped)
+    key_rows = jnp.dot(tokens, wk, preferred_element_type=jnp.float32).astype(jnp.bfloat16).reshape(shaped)
+    value_rows = linear(tokens, wv, value_bias_all).astype(jnp.bfloat16).reshape(shaped)
+    mixed, log_totals = lax.map(attend_forward, (queries, key_rows, value_rows, segment_ids))
+    mixed = mixed.reshape(tokens.shape)
+    first_sum = tokens.astype(jnp.float32) + linear(mixed, wo, out_bias_all)
+    hidden, first_normed, first_rescale = layer_norm(first_sum, gain1, shift1)
+    hidden_low = hidden.astype(jnp.bfloat16)
+    inner = linear(hidden_low, expand_all, expand_bias_all)
+    active = jax.nn.gelu(inner, approximate=False).astype(jnp.bfloat16)
+    second_sum = hidden + linear(active, reduce_all, reduce_bias_all)
+    output, second_normed, second_rescale = layer_norm(second_sum, gain2, shift2)
+    second_grad, grad_second_gain, grad_second_shift = norm_back(
+        cotangent.astype(jnp.float32), second_normed, second_rescale, gain2
+    )
+    branch_grad = second_grad.astype(jnp.bfloat16)
+    grad_reduce = weight_grad(active, branch_grad)
+    grad_reduce_bias = bias_grad(branch_grad)
+    inner_grad = (back_rows(branch_grad, reduce_all) * gelu_slope(inner)).astype(jnp.bfloat16)
+    grad_expand = weight_grad(hidden_low, inner_grad)
+    grad_expand_bias = bias_grad(inner_grad)
+    hidden_grad = second_grad + back_rows(inner_grad, expand_all)
+    expand_own, reduce_own = scatter_all(
+        [
+            grad_expand.astype(low).reshape(LINE, 2, rows, -1),
+            grad_reduce.astype(low).reshape(LINE, 2, -1, width),
+        ],
+        2,
+    )
+    first_grad, grad_first_gain, grad_first_shift = norm_back(
+        hidden_grad, first_normed, first_rescale, gain1
+    )
+    out_grad = first_grad.astype(jnp.bfloat16)
+    grad_out = weight_grad(mixed, out_grad)
+    grad_out_bias = bias_grad(out_grad)
+    mixed_grad = back_rows(out_grad, wo).astype(jnp.bfloat16).reshape(shaped)
+    query_grad, key_grad, value_grad = lax.map(
+        attend_backward, (queries, key_rows, value_rows, segment_ids, mixed_grad, log_totals)
+    )
+    query_grad = query_grad.reshape(tokens.shape)
+    key_grad = key_grad.reshape(tokens.shape)
+    value_grad = value_grad.reshape(tokens.shape)
+    grad_query = weight_grad(tokens, query_grad)
+    grad_query_bias = bias_grad(query_grad)
+    grad_key = weight_grad(tokens, key_grad)
+    grad_value = weight_grad(tokens, value_grad)
+    grad_value_bias = bias_grad(value_grad)
+    input_grad = first_grad + back_rows(query_grad, wq) + back_rows(key_grad, wk) + back_rows(value_grad, wv)
+    small_grads = (
+        grad_query_bias, grad_value_bias, grad_out_bias, grad_first_gain, grad_first_shift,
+        grad_reduce_bias, grad_second_gain, grad_second_shift,
+    )
+    small_grads = jnp.stack(small_grads).reshape(8, shards, rows).transpose(1, 0, 2)
+    small_grads = jnp.concatenate([small_grads, grad_expand_bias.reshape(shards, -1, rows)], axis=1)
+    small_grads = jnp.pad(
+        small_grads.astype(low), ((0, 0), (0, SMALL - small_grads.shape[1]), (0, width - rows))
+    )
+    attention_grads = jnp.concatenate(
+        [g.astype(low).reshape(shards, rows, width) for g in (grad_query, grad_key, grad_value, grad_out)]
+        + [small_grads],
+        axis=1,
+    )
+    (attention_own,) = scatter_all([attention_grads.reshape(LINE, 2, -1, width)], 3)
+    attention_own = attention_own.astype(jnp.float32)
+    small_own = attention_own[4 * rows :, :rows]
+    attention_own = [attention_own[k * rows : (k + 1) * rows] for k in range(4)]
+    return (
+        output.astype(low),
+        input_grad,
+        attention_own[0],
+        small_own[0],
+        attention_own[1],
+        attention_own[2],
+        small_own[1],
+        attention_own[3],
+        small_own[2],
+        small_own[3],
+        small_own[4],
+        expand_own.astype(jnp.float32),
+        small_own[8 : 8 + count // rows].reshape(-1),
+        reduce_own.astype(jnp.float32),
+        small_own[5],
+        small_own[6],
+        small_own[7],
+    )
+
+
 def solution(mesh):
+    fits = mesh.shape["fsdp"] == 2 * LINE and mesh.shape["dp"] == 4
+    body = on_device if fits else plain_on_device
     in_specs = (
         P(("dp", "fsdp"), None),
         P(("dp", "fsdp"), None),
@@ -254,5 +741,5 @@
         P("fsdp"),
     )
     return jax.shard_map(
-        on_device, mesh=mesh, in_specs=in_specs, out_specs=out_specs, check_vma=False
-    )
+        body, mesh=mesh, in_specs=in_specs, out_specs=out_specs, check_vma=False
+    )

time: 755 us -> 531 us (0.70)
  waiting for transfers between devices: 381 us -> 0 us
  Pallas kernels: 0 us -> 244 us
  blocking collectives: 62.2 us -> 0 us
  matrix products: 177 us -> 154 us
  loops' own time: 0.86 us -> 15.7 us
  between operations: 15 us -> 1.61 us
    pallas_call x0 -> x4, Pallas kernels: none -> 244 us  [the longest x2 146 us: scatter_all(): pl.pallas_call(functools.partial(scatter_kernel, len(sources)), out_shape...]
    reduce_scatter x2 -> x0, waiting for transfers between devices: 195 us -> none  [the longest x1 98.9 us: on_device(): lax.psum_scatter(grad_expand.astype(low), 'fsdp', scatter_dimension=0, ti...]
    all_gather x3 -> x0, waiting for transfers between devices: 118 us -> none  [the longest x1 49.7 us: on_device(): attention_all = lax.all_gather(attention_pack, 'fsdp', axis=1, tiled=True)]
    unnamed x8 -> x0, waiting for transfers between devices: 67.4 us -> none
    psum x1 -> x0, blocking collectives: 39.5 us -> none  [on_device(): small_sum = lax.psum(small_sum, ('dp', 'fsdp'))]
    all_gather x1 -> x0, blocking collectives: 22.7 us -> none  [on_device(): gathered_small = lax.all_gather(small_pack, 'fsdp', axis=1, tiled=True)]
    another operation x1, loops' own time: 0.28 us -> 14.8 us  [on_device(): lax.map(attend_forward, (queries, key_rows, value_rows, segment_ids))]
    dot_general x6, matrix products: 43.4 us -> 31.3 us  [back_rows(): jnp.einsum('to,io->ti', gradient, weight, preferred_element_type=jnp.floa...]
  transfers between devices with their start and end apart: 7 -> 0, of which waited for: 6 -> 0; matrix products, arithmetic and copies ran while one was open for 19% -> 0% of each run, Pallas kernels for 0% -> 0%
where the time goes in v2:
time: 531 us; the launch traced here: 527 us
  Pallas kernels  244 us (46%)
  matrix products  154 us (29%)
  local copies, waits for them, and re-layouts  71.5 us (13%)
  other arithmetic  39.8 us (7%)
  loops' own time  15.7 us (3%)
    pallas_call x2, Pallas kernels, scatter_all(): pl.pallas_call(functools.partial(scatter_kernel, len(sources)), out_shape...  146 us
    pallas_call x2, Pallas kernels, gather_all(): pl.pallas_call(functools.partial(gather_kernel, len(shards)), out_shape=[...  98.7 us
    dot_general x5, matrix products, linear(): jnp.dot(rows, weight, preferred_element_type=jnp.float32)  54.8 us
    dot_general x6, matrix products, back_rows(): jnp.einsum('to,io->ti', gradient, weight, preferred_element_type=jnp.floa...  31.3 us
    unnamed x120, local copies, waits for them, and re-layouts  27.8 us
    dot_general x6, matrix products, weight_grad(): jnp.einsum('ti,to->io', rows, gradient, preferred_element_type=jnp.float32)  20.1 us
    another operation x1, loops' own time, on_device(): lax.map(attend_forward, (queries, key_rows, value_rows, segment_ids))  14.8 us
    convert_element_type x2, other arithmetic, attend_backward(): score_grad = (weights * (prob_grad - jnp.sum(prob_grad * weights, axis=-1...  14.2 us

profile of v2, /device:TPU:11, one launch (start us, length us, event | category | flops | bytes accessed | tf_op | source)
XLA Modules:
  0.0 527.1 jit_solution(14962552278328517778)
XLA Ops:
  7.5 36.7 %gather.2 = bf16[8,416,768]{2,1,0:T(8,128)(2,1)} custom-call(bf16[416,768]{1,0:T(8,128)(2,1)} %copy-done.35), custom_call_target="tpu_custom_call" | custom-call | tf_op jit(solution)/shard_map/gather/pallas_call | solution.py:437
  44.2 4.3 fusion.92
  69.9 35.4 %while.26 = (s32[]{:T(128)}, bf16[2,512,12,64]{1,3,2,0:T(8,128)(2,1)}, f32[2,12,512,1]{2,1,3,0:T(8,128)S(1)}, bf16[2,512,12,64]{1,3,2,0:T(8,128)(2,1)}, s32[2,51...) while((s32[]{:T(128)}, ...), condition=%wide.region_4.5_spmd, body=%wide.region_1.4_spmd.sunk | while | flops 843704320 | bytes 42172508 | solution.py:617
  74.8 5.5 %fusion.152 = bf16[2,512,12,64]{1,3,2,0:T(8,128)(2,1)} fusion(bf16[2,512,12,64]{1,3,2,0:T(8,128)(2,1)} %get-tuple-element.430, s32[]{:T(128)} %get-tuple-element.429, f32[12,512,512]{1,2,0:T(8,128)S(1)} %get-tuple-element.407, f32[12,512]{1,0:T(8,128)S(1)} %fusion.151, f32[12,512]{1,0:T(8,128)S(1)} %get-tuple-element.408, ...), kind=kOutput, calls=%fused_computation.8.clone.1 | convolution fusion | flops 418775040 | bytes 14468096 | tf_op jit(solution)/shard_map/while/body/eval_jaxpr/hqk,khd->qhd/dot_general | solution.py:68
  85.2 5.5 %fusion.152 = bf16[2,512,12,64]{1,3,2,0:T(8,128)(2,1)} fusion(bf16[2,512,12,64]{1,3,2,0:T(8,128)(2,1)} %get-tuple-element.430, s32[]{:T(128)} %get-tuple-element.429, f32[12,512,512]{1,2,0:T(8,128)S(1)} %get-tuple-element.407, f32[12,512]{1,0:T(8,128)S(1)} %fusion.151, f32[12,512]{1,0:T(8,128)S(1)} %get-tuple-element.408, ...), kind=kOutput, calls=%fused_computation.8.clone.1 | convolution fusion | flops 418775040 | bytes 14468096 | tf_op jit(solution)/shard_map/while/body/eval_jaxpr/hqk,khd->qhd/dot_general | solution.py:68
  105.4 4.2 copy.89
  113.7 3.8 fusion.94
  118.3 62.0 %gather.3 = (bf16[8,96,3072]{2,1,0:T(8,128)(2,1)}, bf16[8,384,768]{2,1,0:T(8,128)(2,1)}) custom-call(bf16[96,3072]{1,0:T(8,128)(2,1)} %refs_0_.1, bf16[384,768]{1,0:T(8,128)(2,1)} %refs_1_.1), custom_call_target="tpu_custom_call" | custom-call | tf_op jit(solution)/shard_map/gather/pallas_call | solution.py:437
  180.3 37.0 %fusion.59 = (bf16[1024,3072]{1,0:T(8,128)(2,1)S(1)}, f32[1024,3072]{1,0:T(8,128)}) fusion(f32[3072]{0:T(1024)S(1)} %add.164, bf16[768,3072]{1,0:T(8,128)(2,1)} %bitcast.255, f32[1024,768]{0,1:T(8,128)S(1)} %get-tuple-element.299, f32[768]{0:T(1024)S(1)} %get-tuple-element.234, f32[768]{0:T(1024)S(1)} %get-tuple-element.235, f32[1024]{0:T(1024)S(1)} %add_rsqrt_fusion.1, ...), kind=kOutput, calls=%fused_computation.68 | convolution fusion | flops 5043388416 | bytes 26765312 | tf_op jit(solution)/shard_map/dot_general | solution.py:31
  217.3 9.9 %fusion.95 = (f32[1024]{0:T(1024)S(1)}, f32[1024,768]{0,1:T(8,128)S(1)}) fusion(f32[768]{0:T(1024)S(1)} %copy-done.47, bf16[1024,3072]{1,0:T(8,128)(2,1)S(1)} %get-tuple-element.300, bf16[3072,768]{1,0:T(8,128)(2,1)S(1)} %bitcast.258, f32[768]{0:T(1024)S(1)} %get-tuple-element.234, f32[768]{0:T(1024)S(1)} %get-tuple-element.235, ...), kind=kOutput, calls=%fused_computation.180 | convolution fusion | flops 4837342208 | bytes 17323008 | tf_op jit(solution)/shard_map/dot_general | solution.py:31
  230.2 4.4 fusion.79
  236.5 12.8 %fusion.96 = (bf16[3072]{0:T(1024)(128)(2,1)}, bf16[1024,3072]{1,0:T(8,128)(2,1)S(1)}) fusion(f32[1024,3072]{1,0:T(8,128)} %get-tuple-element.301, f32[3072]{0:T(1024)S(1)} %add.164, bf16[1024,768]{0,1:T(8,128)(2,1)S(1)} %get-tuple-element.274, bf16[3072,768]{1,0:T(8,128)(2,1)} %bitcast.257), kind=kOutput, calls=%fused_computation.181 | convolution fusion | flops 4869583872 | bytes 25184256 | tf_op jit(solution)/shard_map/to,io->ti/dot_general | solution.py:43
  249.2 7.3 %convolution_convert_fusion.1 = bf16[768,3072]{1,0:T(8,128)(2,1)} fusion(bf16[1024,3072]{1,0:T(8,128)(2,1)S(1)} %get-tuple-element.306, f32[1024,768]{0,1:T(8,128)S(1)} %copy-done.14, f32[768]{0:T(1024)S(1)} %get-tuple-element.234, f32[768]{0:T(1024)S(1)} %get-tuple-element.235, f32[1024]{0:T(1024)S(1)} %add_rsqrt_fusion.1, ...), kind=kOutput, calls=%fused_computation.91 | convolution fusion | flops 4838129664 | bytes 14170112 | tf_op jit(solution)/shard_map/ti,to->io/dot_general | solution.py:35
  256.5 6.8 %convolution_convert_fusion = bf16[3072,768]{1,0:T(8,128)(2,1)} fusion(bf16[1024,3072]{1,0:T(8,128)(2,1)S(1)} %bitcast.260, bf16[1024,768]{0,1:T(8,128)(2,1)S(1)} %get-tuple-element.274), kind=kOutput, calls=%fused_computation.90 | convolution fusion | flops 4834197504 | bytes 12582912 | tf_op jit(solution)/shard_map/ti,to->io/dot_general | solution.py:35
  263.4 85.5 %scatter_sum.3 = (bf16[96,3072]{1,0:T(8,128)(2,1)}, bf16[384,768]{1,0:T(8,128)(2,1)}) custom-call(bf16[4,2,96,3072]{3,2,1,0:T(8,128)(2,1)} %bitcast.223, bf16[4,2,384,768]{3,2,1,0:T(8,128)(2,1)} %bitcast.224), custom_call_target="tpu_custom_call" | custom-call | tf_op jit(solution)/shard_map/scatter_sum/pallas_call | solution.py:298
  353.4 11.5 %multiply_reduce_fusion.1 = (bf16[768]{0:T(1024)(128)(2,1)}, f32[1024]{0:T(1024)S(1)}, f32[1024]{0:T(1024)S(1)}, bf16[768]{0:T(1024)(128)(2,1)}, f32[1024,768]{0,1:T(8,128)S(1)}) fusion(f32[1024,768]{0,1:T(8,128)} %copy-done.13, f32[1024]{0:T(1024)S(1)} %add_rsqrt_fusion.1, f32[1024]{0:T(1024)S(1)} %broadcast_multiply_fusion.5, ...), kind=kOutput, calls=%fused_computation.101 | convolution fusion | flops 4845989888 | bytes 22062080 | tf_op jit(solution)/shard_map/to,io->ti/dot_general | solution.py:43
  377.2 49.6 %while.27 = (s32[]{:T(128)}, bf16[2,512,12,64]{1,3,2,0:T(8,128)(2,1)}, bf16[2,512,12,64]{1,3,2,0:T(8,128)(2,1)}, bf16[2,512,12,64]{1,3,2,0:T(8,128)(2,1)}, bf16[...) while((s32[]{:T(128)}, ...), condition=%wide.region_15.16_spmd, body=%wide.region_13.15_spmd.sunk | while | flops 2062673920 | bytes 147524944 | solution.py:650
  379.6 6.9 %multiply_reduce_fusion.7 = (f32[12,512]{1,0:T(8,128)S(1)}, f32[12,512,512]{1,2,0:T(8,128)}) fusion(f32[12,512,512]{1,2,0:T(8,128)S(1)} %fusion.161, f32[12,512]{1,0:T(8,128)S(1)} %dynamic-slice_bitcast_fusion.2, pred[512,512]{0,1:T(8,128)(4,1)S(1)} %broadcast_compare_fusion.5, bf16[2,512,12,64]{1,3,2,0:T(8,128)(2,1)S(1)} %copy-done.4, ...), kind=kOutput, calls=%fused_computation.24.clone.1 | convolution fusion | flops 418375680 | bytes 27059200 | tf_op jit(solution)/shard_map/while/body/eval_jaxpr/qhd,khd->hqk/dot_general | solution.py:79
  386.5 7.1 %multiply_convert_fusion.4 = bf16[12,512,512]{1,2,0:T(8,128)(2,1)S(1)} fusion(f32[12,512,512]{1,2,0:T(8,128)} %get-tuple-element.419, f32[12,512,512]{1,2,0:T(8,128)S(1)} %fusion.161, f32[12,512]{1,0:T(8,128)S(1)} %get-tuple-element.420, f32[12,512]{1,0:T(8,128)S(1)} %dynamic-slice_bitcast_fusion.2, pred[512,512]{0,1:T(8,128)(4,1)S(1)} %broadcast_compare_fusion.5), kind=kLoop, calls=%fused_computation.23.clone.1 | loop fusion | flops 18874368 | bytes 31768576 | tf_op jit(solution)/shard_map/while/body/eval_jaxpr/convert_element_type | solution.py:84
  398.0 3.9 fusion.164
  404.0 6.9 %multiply_reduce_fusion.7 = (f32[12,512]{1,0:T(8,128)S(1)}, f32[12,512,512]{1,2,0:T(8,128)}) fusion(f32[12,512,512]{1,2,0:T(8,128)S(1)} %fusion.161, f32[12,512]{1,0:T(8,128)S(1)} %dynamic-slice_bitcast_fusion.2, pred[512,512]{0,1:T(8,128)(4,1)S(1)} %broadcast_compare_fusion.5, bf16[2,512,12,64]{1,3,2,0:T(8,128)(2,1)S(1)} %copy-done.4, ...), kind=kOutput, calls=%fused_computation.24.clone.1 | convolution fusion | flops 418375680 | bytes 27059200 | tf_op jit(solution)/shard_map/while/body/eval_jaxpr/qhd,khd->hqk/dot_general | solution.py:79
  410.9 7.1 %multiply_convert_fusion.4 = bf16[12,512,512]{1,2,0:T(8,128)(2,1)S(1)} fusion(f32[12,512,512]{1,2,0:T(8,128)} %get-tuple-element.419, f32[12,512,512]{1,2,0:T(8,128)S(1)} %fusion.161, f32[12,512]{1,0:T(8,128)S(1)} %get-tuple-element.420, f32[12,512]{1,0:T(8,128)S(1)} %dynamic-slice_bitcast_fusion.2, pred[512,512]{0,1:T(8,128)(4,1)S(1)} %broadcast_compare_fusion.5), kind=kLoop, calls=%fused_computation.23.clone.1 | loop fusion | flops 18874368 | bytes 31768576 | tf_op jit(solution)/shard_map/while/body/eval_jaxpr/convert_element_type | solution.py:84
  422.4 3.9 fusion.164
  449.8 60.0 %scatter_sum.2 = bf16[416,768]{1,0:T(8,128)(2,1)} custom-call(bf16[4,2,416,768]{3,2,1,0:T(8,128)(2,1)} %constant_dynamic-update-slice_fusion.13.refs_0_), custom_call_target="tpu_custom_call" | custom-call | tf_op jit(solution)/shard_map/scatter_sum/pallas_call | solution.py:298
  (245 shorter events, 116.9 us)
Async XLA Ops:
  44.2 7.0 %copy-start.27 = (bf16[1024,768]{1,0:T(8,128)(2,1)S(1)}, bf16[1024,768]{1,0:T(8,128)(2,1)}, u32[]{:S(2)}) copy-start(bf16[1024,768]{1,0:T(8,128)(2,1)} %param.22) | copy-start | bytes 4718596
  105.3 5.8 %copy-start = (bf16[2,512,12,64]{1,3,2,0:T(8,128)(2,1)}, bf16[2,512,12,64]{1,3,2,0:T(8,128)(2,1)S(1)}, u32[]{:S(2)}) copy-start(bf16[2,512,12,64]{1,3,2,0:T(8,128)(2,1)S(1)} %get-tuple-element.478) | copy-start | bytes 4718596
  105.3 5.8 %copy-start.2 = (bf16[2,512,12,64]{1,3,2,0:T(8,128)(2,1)}, bf16[2,512,12,64]{1,3,2,0:T(8,128)(2,1)S(1)}, u32[]{:S(2)}) copy-start(bf16[2,512,12,64]{1,3,2,0:T(8,128)(2,1)S(1)} %get-tuple-element.479) | copy-start | bytes 4718596
  105.3 5.8 %copy-start.36 = (f32[2,12,512,1]{2,1,3,0:T(8,128)}, f32[2,12,512,1]{2,1,3,0:T(8,128)S(1)}, u32[]{:S(2)}) copy-start(f32[2,12,512,1]{2,1,3,0:T(8,128)S(1)} %get-tuple-element.452) | copy-start | bytes 147460
  117.5 99.7 %copy-start.13 = (f32[1024,768]{0,1:T(8,128)}, f32[1024,768]{0,1:T(8,128)S(1)}, u32[]{:S(2)}) copy-start(f32[1024,768]{0,1:T(8,128)S(1)} %get-tuple-element.299) | copy-start | bytes 9437188
  180.3 37.0 %copy-start.47 = (f32[768]{0:T(1024)S(1)}, f32[768]{0:T(1024)}, u32[]{:S(2)}) copy-start(f32[768]{0:T(1024)} %get-tuple-element.233) | copy-start | bytes 9220
  180.3 37.0 %copy-start.50 = (bf16[8,384,768]{2,1,0:T(8,128)(2,1)S(1)}, bf16[8,384,768]{2,1,0:T(8,128)(2,1)}, u32[]{:S(2)}) copy-start(bf16[8,384,768]{2,1,0:T(8,128)(2,1)} %get-tuple-element.115) | copy-start | bytes 14155780
  217.2 9.9 %copy-start.52 = (bf16[1024,3072]{1,0:T(8,128)(2,1)}, bf16[1024,3072]{1,0:T(8,128)(2,1)S(1)}, u32[]{:S(2)}) copy-start(bf16[1024,3072]{1,0:T(8,128)(2,1)S(1)} %get-tuple-element.300) | copy-start | bytes 18874372
  230.2 4.4 copy-start.11
  234.6 21.9 %slice-start.1 = ((s8[6291456]{0:T(1024)(128)(4,1)}), s8[4194304]{0:T(1024)(128)(4,1)S(1)}, s32[]{:S(2)}) async-start(s8[6291456]{0:T(1024)(128)(4,1)} %bitcast.259), calls=%async_computation.1 | async-start | bytes 8388608
  236.4 12.8 %copy-start.14 = (f32[1024,768]{0,1:T(8,128)S(1)}, f32[1024,768]{0,1:T(8,128)}, u32[]{:S(2)}) copy-start(f32[1024,768]{0,1:T(8,128)} %copy-done.13) | copy-start | bytes 9437188
  236.4 20.1 %slice-start.2 = ((s8[6291456]{0:T(1024)(128)(4,1)}), s8[2097152]{0:T(1024)(128)(4,1)S(1)}, s32[]{:S(2)}) async-start(s8[6291456]{0:T(1024)(128)(4,1)} %bitcast.259), calls=%async_computation.2 | async-start | bytes 4194304
  249.2 7.3 %copy-start.51 = (bf16[1024,3072]{1,0:T(8,128)(2,1)}, bf16[1024,3072]{1,0:T(8,128)(2,1)S(1)}, u32[]{:S(2)}) copy-start(bf16[1024,3072]{1,0:T(8,128)(2,1)S(1)} %get-tuple-element.306) | copy-start | bytes 18874372
  348.9 4.5 copy-start.12
  353.4 11.5 %copy-start.15 = (f32[1024,768]{0,1:T(8,128)S(1)}, f32[1024,768]{0,1:T(8,128)}, u32[]{:S(2)}) copy-start(f32[1024,768]{0,1:T(8,128)} %copy-done.13) | copy-start | bytes 9437188
  373.2 4.0 copy-start.40
  386.5 7.1 %copy-start.22 = (bf16[2,512,12,64]{1,3,2,0:T(8,128)(2,1)S(1)}, bf16[2,512,12,64]{1,3,2,0:T(8,128)(2,1)}, u32[]{:S(2)}) copy-start(bf16[2,512,12,64]{1,3,2,0:T(8,128)(2,1)} %get-tuple-element.458) | copy-start | bytes 4718596 | tf_op jit(solution)/shard_map/while
  410.9 7.1 %copy-start.22 = (bf16[2,512,12,64]{1,3,2,0:T(8,128)(2,1)S(1)}, bf16[2,512,12,64]{1,3,2,0:T(8,128)(2,1)}, u32[]{:S(2)}) copy-start(bf16[2,512,12,64]{1,3,2,0:T(8,128)(2,1)} %get-tuple-element.458) | copy-start | bytes 4718596 | tf_op jit(solution)/shard_map/while
  426.8 4.0 copy-start.48
  426.8 4.1 copy-start.43
  426.8 4.2 copy-start.44
  426.8 4.3 copy-start.19
  426.9 4.7 copy-start.46
  426.9 4.8 copy-start.9
  (39 other events, 89.4 us)

commit v3 on v2

--- a/solution.py
+++ b/solution.py
@@ -443,6 +443,154 @@
         compiler_params=pltpu.CompilerParams(collective_id=ident, has_side_effects=True, vmem_limit_bytes=60 * 1024 * 1024),
         name="gather",
     )(*shards)
+
+
+def masked_exp(scores, same):
+    scores = jnp.where(same, scores, -1000000000.0)
+    highest = jnp.max(scores, axis=-1, keepdims=True)
+    return jnp.exp(scores - highest), highest
+
+
+def cross(a, b):
+    return lax.dot_general(a, b, (((1,), (1,)), ((), ())), preferred_element_type=jnp.float32)
+
+
+ROWS = 256
+
+
+def forward_kernel(
+    pack, expand, reduce, tokens, fragment_column, fragment_row,
+    attention_all, expand_all, reduce_all, queries, key_rows, value_rows, mixed, log_totals, normed, rescale,
+    *scratch,
+):
+    rows = pack.shape[0] // 4 - SMALL // 4
+    width = pack.shape[1]
+    count = tokens.shape[0] // ROWS
+    length = fragment_row.shape[2]
+    at = places()
+    greet(at)
+    first = gather_events(at, pack, attention_all, scratch[0:2])
+    second = gather_events(at, expand, expand_all, scratch[2:4])
+    third = gather_events(at, reduce, reduce_all, scratch[4:6])
+    first[0]()
+    for step in first[1]:
+        step()
+    second[0]()
+    third[0]()
+    for step in first[2]:
+        step()
+    log_totals[...] = jnp.zeros_like(log_totals)
+    first[3]()
+
+    def weight(k):
+        return attention_all[:, k * rows : (k + 1) * rows, :].reshape(-1, width)
+
+    vectors = jnp.sum(attention_all[:, 4 * rows : 4 * rows + 16, :].astype(jnp.float32), axis=0)
+
+    def project(i, carry):
+        own = pl.ds(pl.multiple_of(i * ROWS, ROWS), ROWS)
+        some = tokens[own, :]
+        queries[own, :] = (
+            jnp.dot(some, weight(0), preferred_element_type=jnp.float32) + vectors[0:1, :]
+        ).astype(jnp.bfloat16)
+        key_rows[own, :] = jnp.dot(some, weight(1), preferred_element_type=jnp.float32).astype(jnp.bfloat16)
+        value_rows[own, :] = (
+            jnp.dot(some, weight(2), preferred_element_type=jnp.float32) + vectors[1:2, :]
+        ).astype(jnp.bfloat16)
+        return carry
+
+    lax.fori_loop(0, count, project, 0)
+
+    pairs = width // (2 * HEAD)
+    blocks = length // ROWS
+    steps = count * pairs
+    moves = [second[1][0:2], third[1][0:2], second[1][2:4], third[1][2:4], second[1][4:6], third[1][4:6]]
+    when = [0, 4, 9, 14, 19, 23]
+
+    def attend(i, carry):
+        for due, group in zip(when, moves):
+
+            @pl.when(i == due * steps // 24)
+            def _():
+                for step in group:
+                    step()
+
+        pair = lax.rem(i, pairs)
+        block = i // pairs
+        sequence = block // blocks
+        own = pl.ds(pl.multiple_of(block * ROWS, ROWS), ROWS)
+        inside = pl.ds(pl.multiple_of(lax.rem(block, blocks) * ROWS, ROWS), ROWS)
+        every = pl.ds(pl.multiple_of(sequence * length, length), length)
+        lanes = pl.ds(pl.multiple_of(pair * 2 * HEAD, 2 * HEAD), 2 * HEAD)
+        q = queries[own, lanes].astype(jnp.float32) * (HEAD**-0.5)
+        k = key_rows[every, lanes]
+        v = value_rows[every, lanes]
+        same = fragment_column[sequence, inside, :] == fragment_row[sequence]
+        lane = lax.broadcasted_iota(jnp.int32, (ROWS, 2 * HEAD), 1)
+        head_lane = lax.broadcasted_iota(jnp.int32, (ROWS, 128), 1)
+        totals_now = log_totals[own, :]
+        results = []
+        for h in range(2):
+            part = (lane >= HEAD) if h else (lane < HEAD)
+            lifted, highest = masked_exp(cross(jnp.where(part, q, 0.0).astype(jnp.bfloat16), k), same)
+            totals = jnp.sum(lifted, axis=-1, keepdims=True)
+            out = jnp.dot(lifted.astype(jnp.bfloat16), v, preferred_element_type=jnp.float32)
+            results.append(out / totals)
+            totals_now = jnp.where(head_lane == 2 * pair + h, highest + jnp.log(totals), totals_now)
+        mixed[own, lanes] = jnp.where(lane < HEAD, results[0], results[1]).astype(jnp.bfloat16)
+        log_totals[own, :] = totals_now
+        return carry
+
+    lax.fori_loop(0, steps, attend, 0)
+
+    def normalize(i, carry):
+        own = pl.ds(pl.multiple_of(i * ROWS, ROWS), ROWS)
+        total = (
+            tokens[own, :].astype(jnp.float32)
+            + jnp.dot(mixed[own, :], weight(3), preferred_element_type=jnp.float32)
+            + vectors[2:3, :]
+        )
+        centered = total - jnp.mean(total, axis=-1, keepdims=True)
+        scale = lax.rsqrt(jnp.mean(centered * centered, axis=-1, keepdims=True) + 1e-12)
+        normed[own, :] = centered * scale
+        rescale[own, :] = scale
+        return carry
+
+    lax.fori_loop(0, count, normalize, 0)
+    for a, b in zip(second[2], third[2]):
+        a()
+        b()
+    for part in (second, third):
+        part[3]()
+    for part in (first, second, third):
+        part[4]()
+
+
+def forward_all(pack, expand, reduce, tokens, segment_ids):
+    low, full = jnp.bfloat16, jnp.float32
+    count, width = tokens.shape
+    vmem, anywhere = pl.BlockSpec(memory_space=pltpu.VMEM), pl.BlockSpec(memory_space=pl.ANY)
+    shards = 2 * LINE
+    flat = jax.ShapeDtypeStruct(tokens.shape, low)
+    return pl.pallas_call(
+        forward_kernel,
+        out_shape=[
+            jax.ShapeDtypeStruct((shards, *pack.shape), low),
+            jax.ShapeDtypeStruct((shards, *expand.shape), low),
+            jax.ShapeDtypeStruct((shards, *reduce.shape), low),
+            flat, flat, flat, flat,
+            jax.ShapeDtypeStruct((count, 128), full),
+            jax.ShapeDtypeStruct((count, width), full),
+            jax.ShapeDtypeStruct((count, 1), full),
+        ],
+        in_specs=[vmem, anywhere, anywhere, vmem, vmem, vmem],
+        out_specs=[vmem, anywhere, anywhere] + [vmem] * 7,
+        scratch_shapes=gather_scratch() * 3,
+        compiler_params=pltpu.CompilerParams(
+            collective_id=0, has_side_effects=True, vmem_limit_bytes=60 * 1024 * 1024
+        ),
+        name="forward",
+    )(pack, expand, reduce, tokens, segment_ids[:, :, None], segment_ids[:, None, :])
 
 
 def plain_on_device(
@@ -600,24 +748,21 @@
     small = lax.dynamic_update_slice(jnp.zeros((SMALL, width), low), vectors, (0, me * rows))
     small = lax.dynamic_update_slice(small, expand_bias[None, :], (8 + me // per_row, lax.rem(me, per_row) * count))
     pack = jnp.concatenate([query_weight, key_weight, value_weight, out_weight, small], axis=0)
-    (attention_all,) = gather_all([pack], 0)
+    (
+        attention_all, expand_all, reduce_all, queries, key_rows, value_rows, mixed, log_totals, first_normed, first_rescale,
+    ) = forward_all(pack, expand_weight, reduce_weight, tokens, segment_ids)
     wq, wk, wv, wo = [attention_all[:, k * rows : (k + 1) * rows].reshape(width, width) for k in range(4)]
     small_all = jnp.sum(attention_all[:, 4 * rows :].astype(jnp.float32), axis=0)
     query_bias_all, value_bias_all, out_bias_all, gain1, shift1, reduce_bias_all, gain2, shift2 = [
         small_all[k] for k in range(8)
     ]
     expand_bias_all = small_all[8 : 8 + shards // per_row].reshape(-1)
-    expand_all, reduce_all = gather_all([expand_weight, reduce_weight], 1)
     expand_all = expand_all.reshape(width, -1)
     reduce_all = reduce_all.reshape(-1, width)
 
-    queries = linear(tokens, wq, query_bias_all).astype(jnp.bfloat16).reshape(shaped)
-    key_rows = jnp.dot(tokens, wk, preferred_element_type=jnp.float32).astype(jnp.bfloat16).reshape(shaped)
-    value_rows = linear(tokens, wv, value_bias_all).astype(jnp.bfloat16).reshape(shaped)
-    mixed, log_totals = lax.map(attend_forward, (queries, key_rows, value_rows, segment_ids))
-    mixed = mixed.reshape(tokens.shape)
-    first_sum = tokens.astype(jnp.float32) + linear(mixed, wo, out_bias_all)
-    hidden, first_normed, first_rescale = layer_norm(first_sum, gain1, shift1)
+    queries, key_rows, value_rows = [x.reshape(shaped) for x in (queries, key_rows, value_rows)]
+    log_totals = log_totals.reshape(seq_count, seq_length, -1)[:, :, :HEADS].transpose(0, 2, 1)[..., None]
+    hidden = first_normed * gain1 + shift1
     hidden_low = hidden.astype(jnp.bfloat16)
     inner = linear(hidden_low, expand_all, expand_bias_all)
     active = jax.nn.gelu(inner, approximate=False).astype(jnp.bfloat16)

time: 531 us -> 463 us (0.87); the launches traced: 527 us -> 454 us
  matrix products: 154 us -> 125 us
  local copies, waits for them, and re-layouts: 71.5 us -> 56 us
  loops' own time: 15.7 us -> 0.59 us
  Pallas kernels: 244 us -> 235 us
    another operation x1 -> x0, loops' own time: 14.8 us -> none  [on_device(): lax.map(attend_forward, (queries, key_rows, value_rows, segment_ids))]
    unnamed x120 -> x88, local copies, waits for them, and re-layouts: 27.8 us -> 13.3 us
    dot_general x5 -> x2, matrix products: 54.8 us -> 40.5 us  [linear(): jnp.dot(rows, weight, preferred_element_type=jnp.float32)]
    dot_general x3 -> x0, matrix products: 12.4 us -> none  [the longest x2 10.9 us: attend_forward(): jnp.einsum('hqk,khd->qhd', weights, value_rows, preferred_element_type=jn...]
    while x32 -> x28, local copies, waits for them, and re-layouts: 10.1 us -> 2.39 us  [the longest x4 7.73 us: on_device(): lax.map(attend_forward, (queries, key_rows, value_rows, segment_ids))]
    pallas_call x2 -> x1, Pallas kernels: 98.7 us -> 92.4 us  [forward_all(): pl.pallas_call(forward_kernel, out_shape=[jax.ShapeDtypeStruct((shards, *...]
    pallas_call x0 -> x3, local copies, waits for them, and re-layouts: none -> 6.03 us  [forward_all(): pl.pallas_call(forward_kernel, out_shape=[jax.ShapeDtypeStruct((shards, *...]
    reduce_sum x3 -> x0, other arithmetic: 5.44 us -> none  [the longest x2 5.14 us: attend_forward(): totals = jnp.sum(lifted, axis=-1, keepdims=True)]
where the time goes in v3:
time: 463 us; the launch traced here: 454 us
  Pallas kernels  235 us (51%)
  matrix products  125 us (27%)
  local copies, waits for them, and re-layouts  56 us (12%)
  other arithmetic  35 us (8%)
    pallas_call x2, Pallas kernels, scatter_all(): pl.pallas_call(functools.partial(scatter_kernel, len(sources)), out_shape...  143 us
    pallas_call x1, Pallas kernels, forward_all(): pl.pallas_call(forward_kernel, out_shape=[jax.ShapeDtypeStruct((shards, *...  92.4 us
    dot_general x2, matrix products, linear(): jnp.dot(rows, weight, preferred_element_type=jnp.float32)  40.5 us
    dot_general x6, matrix products, back_rows(): jnp.einsum('to,io->ti', gradient, weight, preferred_element_type=jnp.floa...  32.6 us
    dot_general x6, matrix products, weight_grad(): jnp.einsum('ti,to->io', rows, gradient, preferred_element_type=jnp.float32)  20.6 us
    convert_element_type x2, other arithmetic, attend_backward(): score_grad = (weights * (prob_grad - jnp.sum(prob_grad * weights, axis=-1...  14.2 us
    dot_general x2, matrix products, attend_backward(): jnp.einsum('qhd,khd->hqk', mixed_grad, value_rows, preferred_element_type...  13.8 us
    unnamed x88, local copies, waits for them, and re-layouts  13.3 us

profile of v3, /device:TPU:11, one launch (start us, length us, event | category | flops | bytes accessed | tf_op | source)
XLA Modules:
  0.0 453.7 jit_solution(17247305315278749063)
XLA Ops:
  9.7 92.4 %forward.1 = (bf16[8,416,768]{2,1,0:T(8,128)(2,1)}, bf16[8,96,3072]{2,1,0:T(8,128)(2,1)}, bf16[8,384,768]{2,1,0:T(8,128)(2,1)}, bf16[1024,768]{1,0:T(8,128)(2,1)...) custom-call(bf16[416,768]{1,0:T(8,128)(2,1)} %copy-done.23, ...), custom_call_target="tpu_custom_call" | custom-call | tf_op jit(solution)/shard_map/forward/pallas_call | solution.py:575
  103.8 35.1 %fusion.42 = (bf16[1024,3072]{1,0:T(8,128)(2,1)S(1)}, f32[1024,3072]{1,0:T(8,128)}) fusion(f32[3072]{0:T(1024)S(1)} %add.95, bf16[768,3072]{1,0:T(8,128)(2,1)} %bitcast.203, f32[1024,768]{1,0:T(8,128)} %get-tuple-element.83, f32[768]{0:T(1024)S(1)} %get-tuple-element.138, f32[768]{0:T(1024)S(1)} %get-tuple-element.139), kind=kOutput, calls=%fused_computation.45 | convolution fusion | flops 5041815552 | bytes 26757120 | tf_op jit(solution)/shard_map/dot_general | solution.py:31
  138.9 5.4 %fusion.74 = (f32[1024]{0:T(1024)S(1)}, f32[1024,768]{1,0:T(8,128)S(1)}) fusion(f32[768]{0:T(1024)S(1)} %copy-done.33, bf16[1024,3072]{1,0:T(8,128)(2,1)S(1)} %get-tuple-element.184, bf16[3072,768]{1,0:T(8,128)(2,1)S(1)} %bitcast.205, f32[768]{0:T(1024)S(1)} %get-tuple-element.138, f32[1024,768]{1,0:T(8,128)S(1)} %copy-done.13, f32[768]{0:T(1024)S(1)} %get-tuple-element.139), kind=kOutput, calls=%fused_computation.143 | convolution fusion | flops 4835769344 | bytes 17314816 | tf_op jit(solution)/shard_map/dot_general | solution.py:31
  145.7 3.3 fusion.62
  151.1 12.2 %fusion.75 = (bf16[3072]{0:T(1024)(128)(2,1)}, bf16[1024,3072]{1,0:T(8,128)(2,1)S(1)}) fusion(f32[1024,3072]{1,0:T(8,128)} %get-tuple-element.185, f32[3072]{0:T(1024)S(1)} %add.95, bf16[3072,768]{1,0:T(8,128)(2,1)S(1)} %bitcast.206, f32[1024,768]{1,0:T(8,128)S(1)} %get-tuple-element.161), kind=kOutput, calls=%fused_computation.144 | convolution fusion | flops 4870370304 | bytes 26757120 | tf_op jit(solution)/shard_map/to,io->ti/dot_general | solution.py:43
  163.3 7.0 %convolution_convert_fusion.1 = bf16[768,3072]{1,0:T(8,128)(2,1)} fusion(bf16[1024,3072]{1,0:T(8,128)(2,1)S(1)} %get-tuple-element.190, f32[1024,768]{1,0:T(8,128)S(1)} %copy-done.13, f32[768]{0:T(1024)S(1)} %get-tuple-element.138, f32[768]{0:T(1024)S(1)} %get-tuple-element.139), kind=kOutput, calls=%fused_computation.68 | convolution fusion | flops 4836556800 | bytes 14161920 | tf_op jit(solution)/shard_map/ti,to->io/dot_general | solution.py:35
  170.3 7.5 %convolution_convert_fusion = bf16[3072,768]{1,0:T(8,128)(2,1)} fusion(bf16[1024,3072]{1,0:T(8,128)(2,1)S(1)} %get-tuple-element.184, f32[1024,768]{1,0:T(8,128)S(1)} %get-tuple-element.161), kind=kOutput, calls=%fused_computation.67 | convolution fusion | flops 4834983936 | bytes 14155776 | tf_op jit(solution)/shard_map/ti,to->io/dot_general | solution.py:35
  177.8 82.6 %scatter_sum.3 = (bf16[96,3072]{1,0:T(8,128)(2,1)}, bf16[384,768]{1,0:T(8,128)(2,1)}) custom-call(bf16[4,2,96,3072]{3,2,1,0:T(8,128)(2,1)} %bitcast.175, bf16[4,2,384,768]{3,2,1,0:T(8,128)(2,1)} %bitcast.176), custom_call_target="tpu_custom_call" | custom-call | tf_op jit(solution)/shard_map/scatter_sum/pallas_call | solution.py:298
  264.9 10.9 %multiply_reduce_fusion.1 = (bf16[768]{0:T(1024)(128)(2,1)}, f32[1024]{0:T(1024)S(1)}, f32[1024]{0:T(1024)S(1)}, bf16[768]{0:T(1024)(128)(2,1)}, f32[1024,768]{1,0:T(8,128)}) fusion(f32[1024,768]{1,0:T(8,128)S(1)} %copy-done.14, f32[768]{0:T(1024)S(1)} %get-tuple-element.139, f32[1024,768]{1,0:T(8,128)S(1)} %get-tuple-element.161, ...), kind=kOutput, calls=%fused_computation.78 | convolution fusion | flops 4838125568 | bytes 20461568 | tf_op jit(solution)/shard_map/to,io->ti/dot_general | solution.py:43
  276.1 4.1 convert_reduce_fusion.1
  292.8 2.4 reshape.197
  296.9 2.6 copy.68
  299.5 3.9 reshape.201
  303.4 2.9 copy.72
  307.5 49.3 %while.14 = (s32[]{:T(128)}, bf16[2,512,12,64]{1,3,2,0:T(8,128)(2,1)}, bf16[2,512,12,64]{1,3,2,0:T(8,128)(2,1)}, bf16[2,512,12,64]{1,3,2,0:T(8,128)(2,1)}, bf16[...) while((s32[]{:T(128)}, ...), condition=%wide.region_9.10_spmd, body=%wide.region_7.9_spmd.sunk | while | flops 2062673920 | bytes 147524944 | solution.py:795
  309.8 6.9 %multiply_reduce_fusion.6 = (f32[12,512]{1,0:T(8,128)S(1)}, f32[12,512,512]{1,2,0:T(8,128)}) fusion(f32[12,512,512]{1,2,0:T(8,128)S(1)} %fusion.122, f32[12,512]{1,0:T(8,128)S(1)} %dynamic-slice_bitcast_fusion.2, pred[512,512]{0,1:T(8,128)(4,1)S(1)} %broadcast_compare_fusion.2, bf16[2,512,12,64]{1,3,2,0:T(8,128)(2,1)S(1)} %copy-done.2, ...), kind=kOutput, calls=%fused_computation.1.clone.1 | convolution fusion | flops 418375680 | bytes 27059200 | tf_op jit(solution)/shard_map/while/body/eval_jaxpr/qhd,khd->hqk/dot_general | solution.py:79
  316.7 7.1 %multiply_convert_fusion.4 = bf16[12,512,512]{1,2,0:T(8,128)(2,1)S(1)} fusion(f32[12,512,512]{1,2,0:T(8,128)} %get-tuple-element.256, f32[12,512,512]{1,2,0:T(8,128)S(1)} %fusion.122, f32[12,512]{1,0:T(8,128)S(1)} %get-tuple-element.257, f32[12,512]{1,0:T(8,128)S(1)} %dynamic-slice_bitcast_fusion.2, pred[512,512]{0,1:T(8,128)(4,1)S(1)} %broadcast_compare_fusion.2), kind=kLoop, calls=%fused_computation.clone.1 | loop fusion | flops 18874368 | bytes 31768576 | tf_op jit(solution)/shard_map/while/body/eval_jaxpr/convert_element_type | solution.py:84
  328.2 3.9 fusion.125
  334.3 6.9 %multiply_reduce_fusion.6 = (f32[12,512]{1,0:T(8,128)S(1)}, f32[12,512,512]{1,2,0:T(8,128)}) fusion(f32[12,512,512]{1,2,0:T(8,128)S(1)} %fusion.122, f32[12,512]{1,0:T(8,128)S(1)} %dynamic-slice_bitcast_fusion.2, pred[512,512]{0,1:T(8,128)(4,1)S(1)} %broadcast_compare_fusion.2, bf16[2,512,12,64]{1,3,2,0:T(8,128)(2,1)S(1)} %copy-done.2, ...), kind=kOutput, calls=%fused_computation.1.clone.1 | convolution fusion | flops 418375680 | bytes 27059200 | tf_op jit(solution)/shard_map/while/body/eval_jaxpr/qhd,khd->hqk/dot_general | solution.py:79
  341.2 7.1 %multiply_convert_fusion.4 = bf16[12,512,512]{1,2,0:T(8,128)(2,1)S(1)} fusion(f32[12,512,512]{1,2,0:T(8,128)} %get-tuple-element.256, f32[12,512,512]{1,2,0:T(8,128)S(1)} %fusion.122, f32[12,512]{1,0:T(8,128)S(1)} %get-tuple-element.257, f32[12,512]{1,0:T(8,128)S(1)} %dynamic-slice_bitcast_fusion.2, pred[512,512]{0,1:T(8,128)(4,1)S(1)} %broadcast_compare_fusion.2), kind=kLoop, calls=%fused_computation.clone.1 | loop fusion | flops 18874368 | bytes 31768576 | tf_op jit(solution)/shard_map/while/body/eval_jaxpr/convert_element_type | solution.py:84
  352.6 3.9 fusion.125
  379.7 60.0 %scatter_sum.2 = bf16[416,768]{1,0:T(8,128)(2,1)} custom-call(bf16[4,2,416,768]{3,2,1,0:T(8,128)(2,1)} %constant_dynamic-update-slice_fusion.13.refs_0_), custom_call_target="tpu_custom_call" | custom-call | tf_op jit(solution)/shard_map/scatter_sum/pallas_call | solution.py:298
  444.9 3.3 fusion.76
  450.0 3.2 add_add_fusion
  (193 shorter events, 76.7 us)
Async XLA Ops:
  6.6 3.0 copy-start.23
  103.8 35.1 %copy-start.13 = (f32[1024,768]{1,0:T(8,128)S(1)}, f32[1024,768]{1,0:T(8,128)}, u32[]{:S(2)}) copy-start(f32[1024,768]{1,0:T(8,128)} %get-tuple-element.83) | copy-start | bytes 9437188
  103.8 35.1 %copy-start.33 = (f32[768]{0:T(1024)S(1)}, f32[768]{0:T(1024)}, u32[]{:S(2)}) copy-start(f32[768]{0:T(1024)} %get-tuple-element.137) | copy-start | bytes 9220
  103.8 35.1 %copy-start.36 = (bf16[8,384,768]{2,1,0:T(8,128)(2,1)S(1)}, bf16[8,384,768]{2,1,0:T(8,128)(2,1)}, u32[]{:S(2)}) copy-start(bf16[8,384,768]{2,1,0:T(8,128)(2,1)} %get-tuple-element.86) | copy-start | bytes 14155780
  163.3 7.0 %copy-start.38 = (bf16[1024,3072]{1,0:T(8,128)(2,1)}, bf16[1024,3072]{1,0:T(8,128)(2,1)S(1)}, u32[]{:S(2)}) copy-start(bf16[1024,3072]{1,0:T(8,128)(2,1)S(1)} %get-tuple-element.190) | copy-start | bytes 18874372
  260.4 4.5 copy-start.14
  264.9 10.9 %copy-start.24 = (f32[1024,1]{1,0:T(8,128)S(1)}, f32[1024,1]{1,0:T(8,128)}, u32[]{:S(2)}) copy-start(f32[1024,1]{1,0:T(8,128)} %get-tuple-element.87) | copy-start | bytes 12292
  275.9 4.3 slice-start
  276.1 4.2 slice-start.1
  280.1 2.8 copy-start.3
  299.5 8.0 %copy-start.25 = (s32[2,512]{1,0:T(2,128)S(1)}, s32[2,512]{1,0:T(2,128)}, u32[]{:S(2)}) copy-start(s32[2,512]{1,0:T(2,128)} %param.21) | copy-start | bytes 12292
  316.7 7.1 %copy-start.19 = (bf16[2,512,12,64]{1,3,2,0:T(8,128)(2,1)S(1)}, bf16[2,512,12,64]{1,3,2,0:T(8,128)(2,1)}, u32[]{:S(2)}) copy-start(bf16[2,512,12,64]{1,3,2,0:T(8,128)(2,1)} %get-tuple-element.271) | copy-start | bytes 4718596 | tf_op jit(solution)/shard_map/while
  341.2 7.1 %copy-start.19 = (bf16[2,512,12,64]{1,3,2,0:T(8,128)(2,1)S(1)}, bf16[2,512,12,64]{1,3,2,0:T(8,128)(2,1)}, u32[]{:S(2)}) copy-start(bf16[2,512,12,64]{1,3,2,0:T(8,128)(2,1)} %get-tuple-element.271) | copy-start | bytes 4718596 | tf_op jit(solution)/shard_map/while
  356.8 3.8 copy-start.31
  356.8 3.9 copy-start.35
  356.8 4.0 copy-start.34
  356.8 4.1 copy-start.30
  356.8 4.1 copy-start.28
  356.8 4.2 copy-start.29
  356.8 4.3 copy-start.32
  356.9 4.5 copy-start.9
  372.7 3.3 copy-start.37
  444.9 3.3 copy-start.18
  444.9 3.4 copy-start.22
  (24 other events, 43.6 us)
